TPU v7x, 512 devices: a whole 4x4x16 slice. The times are simulated.
512 devices in a mesh: dp: 16 (over z_hi, x), shard: 32 (over y, z_lo, core).
Axes of the slice: x: 4, y: 4, z: 16 (z_hi: 4, z_lo: 4; z = z_hi * 4 + z_lo), core: 2. Of those that a mesh axis runs over, the one named last changes fastest.
Arguments:
- inputs: bfloat16 [2, 4096, 8192], P(None, 'dp', 'shard'), may hold values from -6 to 6
- key_panel: bfloat16 [8192, 4096], P('dp', 'shard'), may hold values from -0.0625 to 0.0625
- value_panel: bfloat16 [8192, 4096], P('dp', 'shard'), may hold values from -0.0625 to 0.0625
- short_filters: float32 [2, 4096, 7], P(None, 'shard'), may hold values from -2 to 2
- medium_filters: float32 [256, 128], P('shard'), may hold values from -0.5 to 0.5
- lengths: int32 [2], replicated, may hold values from 2048 to 4096, as said below
- cotangent: bfloat16 [2, 4096, 4096], P(None, 'dp', 'shard'), may hold values from -0.099609375 to 0.099609375
Outputs:
- mixed: bfloat16 [2, 4096, 4096], P(None, 'dp', 'shard')
- key_grad: bfloat16 [8192, 4096], P('dp', 'shard')
- value_grad: bfloat16 [8192, 4096], P('dp', 'shard')
- short_grad: float32 [2, 4096, 7], P(None, 'shard')
- medium_grad: float32 [256, 128], P('shard')
Inputs may be any that keep to these rules, and one draw needn't show every extreme that they name: `lengths`: each length is a multiple of 16; one window in every draw has the full length 4096, the others are shorter.
All inputs are finite; a program needn't handle non-finite values.
Results may differ from a plain program's by a relative error of at most 0.014.
Values may be sent and summed in bfloat16 or wider, within the bound.
No kernel may reach another device: no remote copies, remote signals or barrier semaphores. Data moves between devices by JAX's collectives and lax.ppermute only.
A program may use at most 64 MiB of HBM per device.

v0:
```python
import functools

import jax
import jax.numpy as jnp
from jax import lax
from jax.experimental import pallas as pl
from jax.experimental.pallas import tpu as pltpu
from jax.sharding import PartitionSpec as P


BF = jnp.bfloat16
F32 = jnp.float32


def dp_move(value, dzh, dx):
    pairs = [
        (zh * 4 + x, ((zh + dzh) % 4) * 4 + (x + dx) % 4) for zh in range(4) for x in range(4)
    ]
    return lax.ppermute(value, "dp", pairs)


def shifted(value, steps):
    first, last = (max(0, -steps), min(16, 16 - steps))
    return lax.ppermute(value, "dp", [(i, i + steps) for i in range(first, last)])


def gather_panels(block):
    half = block.shape[0] // 2
    up = dp_move(block, 1, 0)
    down = dp_move(block, -1, 0)
    far_up = dp_move(up[:half], 1, 0)
    far_down = dp_move(down[half:], -1, 0)
    near = jnp.stack([block, up, down])
    far = jnp.concatenate([far_up, far_down])[None]
    east = dp_move(near, 0, 1)
    west = dp_move(near, 0, -1)
    east_far = dp_move(far, 0, 1)
    west_far = dp_move(far, 0, -1)
    two_east = dp_move(east[:2], 0, 1)
    two_west = dp_move(jnp.concatenate([west[2:], west_far]), 0, -1)
    return near, far, east, east_far, west, west_far, two_east, two_west


W_PIECES = ((0, 0), (0, 3), (3, 0), (3, 3), (1, 0), (1, 3), (2, 0), (2, 2))
ZH_REL = (0, 3, 1, 2)


def forward_kernel(idx_ref, x_ref, *refs):
    w_refs, (out_ref, head_ref, x_buf, w_buf, x_sem, w_sem) = refs[:8], refs[8:]
    blocks, rows, depth = x_ref.shape
    for block in range(blocks):
        pltpu.make_async_copy(
            x_ref.at[block], x_buf.at[:, block * depth : (block + 1) * depth], x_sem.at[block]
        ).start()
    for piece, ref in enumerate(w_refs):
        rel, first = W_PIECES[piece]
        for k in range(ref.shape[0]):
            slot = lax.rem(idx_ref[0] + ZH_REL[first + k], 4) * 4 + lax.rem(idx_ref[1] + rel, 4)
            pltpu.make_async_copy(ref.at[k], w_buf.at[slot], w_sem.at[slot]).start()
    total = jnp.zeros((rows, w_buf.shape[2]), F32)
    for part in range(4):
        for block in range(8 * part, 8 * part + 8):
            pltpu.make_async_copy(
                x_ref.at[0], x_buf.at[:, block * depth : (block + 1) * depth], x_sem.at[block]
            ).wait()
        for slot in range(4 * part, 4 * part + 4):
            pltpu.make_async_copy(w_refs[0].at[0], w_buf.at[slot], w_sem.at[slot]).wait()
        weights = w_buf[4 * part : 4 * part + 4].reshape(8 * depth, w_buf.shape[2])
        total = total + jnp.dot(
            x_buf[:, 8 * part * depth : 8 * (part + 1) * depth],
            weights,
            preferred_element_type=F32,
        )
    turned = total.T.astype(BF)
    out_ref[...] = turned
    half = turned.shape[1] // 2
    head_ref[:, :128] = turned[:, :128]
    head_ref[:, 128:] = turned[:, half : half + 128]


def forward_matmul(idx, features, panels):
    blocks, rows, depth = features.shape
    width = panels[0].shape[2]
    return pl.pallas_call(
        forward_kernel,
        out_shape=[
            jax.ShapeDtypeStruct((width, rows), BF),
            jax.ShapeDtypeStruct((width, 256), BF),
        ],
        in_specs=[
            pl.BlockSpec(memory_space=pltpu.SMEM),
            pl.BlockSpec(memory_space=pltpu.HBM),
        ]
        + [pl.BlockSpec(memory_space=pl.ANY)] * 8,
        out_specs=[pl.BlockSpec(memory_space=pltpu.VMEM)] * 2,
        scratch_shapes=[
            pltpu.VMEM((rows, blocks * depth), BF),
            pltpu.VMEM((blocks // 2, 2 * depth, width), BF),
            pltpu.SemaphoreType.DMA((blocks,)),
            pltpu.SemaphoreType.DMA((blocks // 2,)),
        ],
        compiler_params=pltpu.CompilerParams(vmem_limit_bytes=40 << 20),
    )(idx, features, *panels)


GROUPS = ((2,), (1, 3, 0))
HALF = 128
SMALL = 32


def split(value):
    high = value.astype(BF)
    return high, (value - high.astype(F32)).astype(BF)


def joined(message):
    return message[:, :128].astype(F32) + message[:, 128:256].astype(F32)


def put_small(ref, first, value):
    high, rest = split(value)
    ref[first : first + SMALL, 0:128] = high
    ref[first : first + SMALL, 128:256] = rest
    ref[first : first + SMALL, 256:512] = jnp.zeros((SMALL, 256), BF)


def ring_sum(own, before, after, opposite):
    high, rest = split(own)
    return (high.astype(F32) + rest.astype(F32) + joined(opposite)) + (joined(before) + joined(after))


def small_rows(value):
    return jnp.concatenate([*split(value), jnp.zeros((SMALL, 256), BF)], axis=1)


def backward_kernel(rels, idx_ref, x_ref, grad_ref, *refs):
    east, west, keep_e, keep_w, own, x_buf, x_sem = refs[-7:]
    count, depth = len(rels), x_buf.shape[2]
    order = [(rel_x, k, rel) for rel_x in (2, 1, 3, 0) for k, rel in enumerate(rels)]
    copies = []
    for place, (rel_x, _, rel) in enumerate(order):
        slot = lax.rem(idx_ref[0] + rel, 4) * 8 + lax.rem(idx_ref[1] + rel_x, 4) * 2
        copy = pltpu.make_async_copy(
            x_ref.at[pl.ds(slot, 2)], x_buf.at[pl.ds(2 * place, 2)], x_sem.at[place]
        )
        copy.start()
        copies.append(copy)
    if count == 1:
        for ref in (east, west):
            put_small(ref, 2 * HALF, refs[0][...])
    grad = grad_ref[...]
    for place, (rel_x, k, _) in enumerate(order):
        first = slice(k * HALF, (k + 1) * HALF)
        second = slice((count + k) * HALF, (count + k + 1) * HALF)
        low_to, high_to = {
            2: ((east, first), (west, first)),
            1: ((keep_e, first), (east, second)),
            3: ((west, second), (keep_w, first)),
            0: ((own, first), (own, second)),
        }[rel_x]
        copies[place].wait()
        for core in range(2):
            columns = slice(core * depth, (core + 1) * depth)
            part = jnp.dot(grad, x_buf[2 * place + core], preferred_element_type=F32).astype(BF)
            low_to[0][low_to[1], columns] = part[:HALF]
            high_to[0][high_to[1], columns] = part[HALF:]


def backward_matmul(rels, idx, features, grad, *small):
    _, rows, depth = features.shape
    count = len(rels)
    one = jax.ShapeDtypeStruct((count * HALF, 2 * depth), BF)
    two = jax.ShapeDtypeStruct((2 * count * HALF, 2 * depth), BF)
    sent = jax.ShapeDtypeStruct((2 * count * HALF + SMALL * len(small), 2 * depth), BF)
    return pl.pallas_call(
        functools.partial(backward_kernel, rels),
        out_shape=[sent, sent, one, one, two],
        in_specs=[
            pl.BlockSpec(memory_space=pltpu.SMEM),
            pl.BlockSpec(memory_space=pltpu.HBM),
        ]
        + [pl.BlockSpec(memory_space=pltpu.VMEM)] * (1 + len(small)),
        out_specs=[pl.BlockSpec(memory_space=pltpu.VMEM)] * 5,
        scratch_shapes=[
            pltpu.VMEM((8 * count, rows, depth), BF),
            pltpu.SemaphoreType.DMA((4 * count,)),
        ],
        compiler_params=pltpu.CompilerParams(vmem_limit_bytes=40 << 20),
    )(idx, features, grad, *small)


def add(*terms):
    total = terms[0].astype(F32)
    for term in terms[1:]:
        total = total + term.astype(F32)
    return total


def ring_first(parts):
    return dp_move(parts[0], 0, 1), dp_move(parts[1], 0, -1)


def ring_second(parts, received):
    _, _, keep_e, keep_w, _ = parts
    from_west, from_east = received
    rows = keep_e.shape[0]
    east = add(keep_e, from_west[:rows]).astype(BF)
    west = add(keep_w, from_east[:rows]).astype(BF)
    if from_west.shape[0] > 2 * rows:
        east = jnp.concatenate([east, from_west[2 * rows :]])
    return dp_move(east, 0, 1), dp_move(west, 0, -1)


def reduce_grads(idx, features, outgoing, small):
    far = backward_matmul(GROUPS[0], idx, features, outgoing, small)
    from_west, from_east = far_first = ring_first(far)
    near = backward_matmul(GROUPS[1], idx, features, outgoing)
    near_first = ring_first(near)
    east2, west2 = ring_second(far, far_first)
    low = add(far[4][:HALF], from_east[HALF : 2 * HALF], east2[:HALF]).astype(BF)
    high = add(far[4][HALF:], from_west[HALF : 2 * HALF], west2).astype(BF)
    small = ring_sum(small, from_west[2 * HALF :], from_east[2 * HALF :], east2[HALF:])
    row = small_rows(small)
    from_south = dp_move(jnp.concatenate([low, row]), 1, 0)
    from_north = dp_move(jnp.concatenate([high, row]), -1, 0)
    east2, west2 = ring_second(near, near_first)
    from_west, from_east = near_first
    low = add(near[4][: 3 * HALF], from_east[3 * HALF :], east2)
    high = add(near[4][3 * HALF :], from_west[3 * HALF :], west2)
    north = jnp.concatenate(
        [
            add(low[:HALF], from_south[:HALF]).astype(BF),
            high[:HALF].astype(BF),
            from_south[HALF:],
        ]
    )
    south = jnp.concatenate(
        [low[HALF : 2 * HALF].astype(BF), add(high[HALF : 2 * HALF], from_north[:HALF]).astype(BF)]
    )
    north2, south2 = dp_move(north, 1, 0), dp_move(south, -1, 0)
    small = ring_sum(small, from_south[HALF:], from_north[HALF:], north2[2 * HALF :])
    key = add(low[2 * HALF :], north2[:HALF], south2[:HALF]).astype(BF).T
    value = add(high[2 * HALF :], north2[HALF : 2 * HALF], south2[HALF:]).astype(BF).T
    return key, value, small


def toeplitz(row):
    spread = jnp.broadcast_to(row, (256, 256))
    return pltpu.roll(spread, 0, 1, stride=1, stride_axis=0)[:, :128].astype(BF)


def cotangent_kernel(meta_ref, own_ref, next_ref, ahead_ref, behind_ref, up_ref, grad_ref, band_ref, ext):
    for s in range(2):
        base = meta_ref[0]
        place = lax.broadcasted_iota(jnp.int32, (128, 256), 1) + base
        own = own_ref[s].astype(F32).T
        own = jnp.where(place < meta_ref[1 + s], own, 0.0).astype(BF)
        up_ref[:, s * 256 : (s + 1) * 256] = own
        tail = jnp.concatenate([next_ref[s].astype(F32), jnp.zeros((112, 128), F32)]).T
        tail = jnp.where(place + 256 < meta_ref[1 + s], tail, 0.0).astype(BF)
        ext[:, s * 512 : s * 512 + 256] = own
        ext[:, s * 512 + 256 : (s + 1) * 512] = tail
    for g in range(8):
        band_ref[g] = toeplitz(behind_ref[g : g + 1])
        rows = slice(16 * g, 16 * g + 16)
        left = jnp.concatenate(
            [
                ext[rows, s * 512 + 128 * b : s * 512 + 128 * b + 256]
                for s in range(2)
                for b in range(3)
            ]
        )
        total = jnp.dot(left, toeplitz(ahead_ref[g : g + 1]), preferred_element_type=F32)
        for part in range(6):
            grad_ref[rows, part * 128 : part * 128 + 128] = total[part * 16 : part * 16 + 16]


def cotangent_terms(meta, own, after, medium):
    zeros = jnp.zeros((8, 128), F32)
    ahead = jnp.concatenate([medium[:, :1], zeros, medium[:, :0:-1]], axis=1)
    behind = jnp.concatenate([zeros, medium], axis=1)
    return pl.pallas_call(
        cotangent_kernel,
        out_shape=[
            jax.ShapeDtypeStruct((128, 512), BF),
            jax.ShapeDtypeStruct((128, 768), F32),
            jax.ShapeDtypeStruct((8, 256, 128), BF),
        ],
        in_specs=[pl.BlockSpec(memory_space=pltpu.SMEM)] + [pl.BlockSpec(memory_space=pltpu.VMEM)] * 4,
        out_specs=[pl.BlockSpec(memory_space=pltpu.VMEM)] * 3,
        scratch_shapes=[pltpu.VMEM((128, 1024), BF)],
    )(meta, own, after, ahead, behind)


def middle_kernel(
    kv_ref, prev_ref, head_ref, grad_ref, taps_ref, dy_ref, prod_ref, sums_ref
):
    lanes = lax.broadcasted_iota(jnp.int32, (128, 128), 1)
    sums = jnp.zeros((128, 128), F32)
    partial = [[None] * 7 for _ in range(2)]
    for s in range(2):
        smooth = []
        for b in range(2):
            rows = slice(128 * b, 128 * b + 128)
            ext = jnp.concatenate(
                [
                    prev_ref[rows, s * 256 : (s + 1) * 256],
                    kv_ref[rows, s * 256 : (s + 1) * 256],
                    head_ref[rows, s * 128 : (s + 1) * 128],
                ],
                axis=1,
            ).astype(F32)
            total = taps_ref[rows, 0:1] * ext
            for j in range(1, 7):
                total = total + taps_ref[rows, j : j + 1] * pltpu.roll(ext, j, 1)
            smooth.append(total[:, 128:])
        prod_ref[:, s * 384 : (s + 1) * 384] = (smooth[0][:, :384] * smooth[1][:, :384]).astype(BF)
        for b in range(2):
            rows = slice(128 * b, 128 * b + 128)
            slope = grad_ref[:, s * 384 : (s + 1) * 384] * smooth[1 - b][:, 128:512]
            own = kv_ref[rows, s * 256 : (s + 1) * 256].astype(F32)
            act = jnp.zeros((128, 256), F32)
            for j in range(7):
                moved = (slope if j == 0 else pltpu.roll(slope, 384 - j, 1))[:, :256]
                act = act + taps_ref[rows, j : j + 1] * moved
                both = moved * own
                both = both[:, :128] + both[:, 128:]
                partial[b][j] = both if s == 0 else partial[b][j] + both
            dy_ref[rows, s * 256 : (s + 1) * 256] = act.astype(BF)
    for b in range(2):
        for j in range(7):
            column = jnp.sum(partial[b][j], axis=1, keepdims=True)
            sums = jnp.where(lanes == b * 8 + j, column, sums)
    sums_ref[...] = sums.T[0:16]


def middle_terms(kv, prev, head, grad, short_filters):
    taps = jnp.pad(short_filters.reshape(256, 7), ((0, 0), (0, 1)))
    return pl.pallas_call(
        middle_kernel,
        out_shape=[
            jax.ShapeDtypeStruct((256, 512), BF),
            jax.ShapeDtypeStruct((128, 768), BF),
            jax.ShapeDtypeStruct((16, 128), F32),
        ],
        in_specs=[pl.BlockSpec(memory_space=pltpu.VMEM)] * 5,
        out_specs=[pl.BlockSpec(memory_space=pltpu.VMEM)] * 3,
    )(kv, prev, head, grad, taps)


def response_kernel(meta_ref, prod, up_ref, band_ref, sums_ref, mixed_ref, small_ref, resp):
    small_ref[0:16] = sums_ref[...]
    for g in range(8):
        rows = slice(16 * g, 16 * g + 16)
        left = jnp.concatenate(
            [
                prod[rows, s * 384 + 128 * b : s * 384 + 128 * b + 256]
                for s in range(2)
                for b in range(2)
            ]
        )
        total = jnp.dot(left, band_ref[g], preferred_element_type=F32)
        for part in range(4):
            resp[rows, part * 128 : part * 128 + 128] = total[part * 16 : part * 16 + 16]
        above = jnp.concatenate(
            [up_ref[rows, part * 128 : part * 128 + 128] for part in range(4)]
        )
        folded = lax.dot_general(
            above, left, (((0,), (0,)), ((), ())), preferred_element_type=F32
        )
        count = 64
        while count >= 1:
            folded = folded[:count] + pltpu.roll(folded[count : 2 * count], 256 - count, 1)
            count //= 2
        small_ref[16 + g : 17 + g] = folded[:, :128]
        small_ref[24 + g : 25 + g] = folded[:, 128:]
    for s in range(2):
        place = lax.broadcasted_iota(jnp.int32, (256, 128), 0) + meta_ref[0]
        turned = resp[:, s * 256 : (s + 1) * 256].T
        mixed_ref[s] = jnp.where(place < meta_ref[1 + s], turned, 0.0).astype(BF)


def response_terms(meta, prod, up, bands, sums):
    return pl.pallas_call(
        response_kernel,
        out_shape=[
            jax.ShapeDtypeStruct((2, 256, 128), BF),
            jax.ShapeDtypeStruct((32, 128), F32),
        ],
        in_specs=[pl.BlockSpec(memory_space=pltpu.SMEM)] + [pl.BlockSpec(memory_space=pltpu.VMEM)] * 4,
        out_specs=[pl.BlockSpec(memory_space=pltpu.VMEM)] * 2,
        scratch_shapes=[pltpu.VMEM((128, 512), F32)],
    )(meta, prod, up, bands, sums)


def body(inputs, key_panel, value_panel, short_filters, medium_filters, lengths, cotangent):
    seqs, count, local_width = inputs.shape
    channels = key_panel.shape[1]
    dp = lax.axis_index("dp")
    idx = jnp.stack([dp // 4, dp % 4]).astype(jnp.int32)
    meta = jnp.concatenate([(dp * count).reshape(1).astype(jnp.int32), lengths])

    features = lax.all_gather(inputs.reshape(seqs * count, local_width), "shard", axis=0)
    features = pltpu.with_memory_space_constraint(features, pltpu.HBM)
    panels = gather_panels(jnp.concatenate([key_panel, value_panel], axis=1))
    after = shifted(cotangent[:, :144], -1)
    up, product_grad, bands = cotangent_terms(meta, cotangent, after, medium_filters)

    kv, head = forward_matmul(idx, features, panels)
    prev = shifted(kv, 1)
    head = shifted(head, -1)
    outgoing, product, sums = middle_terms(kv, prev, head, product_grad, short_filters)

    mixed, small = response_terms(meta, product, up, bands, sums)
    key_grad, value_grad, small = reduce_grads(idx, features, outgoing, small)
    short_grad = small[:16].reshape(2, 8, channels)[:, :7].transpose(0, 2, 1)
    medium_grad = jnp.concatenate([small[24:, :1], small[16:24, :0:-1]], axis=1)
    return (mixed, key_grad, value_grad, short_grad, medium_grad)


def solution(mesh):
    return jax.shard_map(
        body,
        mesh=mesh,
        in_specs=(
            P(None, "dp", "shard"),
            P("dp", "shard"),
            P("dp", "shard"),
            P(None, "shard", None),
            P("shard", None),
            P(),
            P(None, "dp", "shard"),
        ),
        out_specs=(
            P(None, "dp", "shard"),
            P("dp", "shard"),
            P("dp", "shard"),
            P(None, "shard", None),
            P("shard", None),
        ),
        check_vma=False,
    )
```

profile of v0, /device:TPU:32, one launch (start us, length us, event | category | flops | bytes accessed | tf_op | source)
XLA Modules:
  0.0 271.4 jit_solution(4485444425561403623)
XLA Ops:
  9.8 9.1 %collective-permute-start = (bf16[512,256]{1,0:T(8,128)(2,1)S(1)}, bf16[512,256]{1,0:T(8,128)(2,1)S(1)}, u32[]{:S(2)}, u32[]{:S(2)}) collective-permute-start(bf16[512,256]{1,0:T(8,128)(2,1)S(1)} %constant_dynamic-update-slice_fusion), channel_id=1, source_target_pairs={{0,128},{32,160},{64,192},{96,224},{128,256},{160,288},{192,320},{... | collective-permute-start | bytes 786440 | tf_op jit(solution)/shard_map/ppermute | solution.py:19
  18.9 4.7 %collective-permute-start.1 = (bf16[512,256]{1,0:T(8,128)(2,1)S(1)}, bf16[512,256]{1,0:T(8,128)(2,1)S(1)}, u32[]{:S(2)}, u32[]{:S(2)}) collective-permute-start(bf16[512,256]{1,0:T(8,128)(2,1)S(1)} %constant_dynamic-update-slice_fusion), channel_id=1, source_target_pairs={{0,384},{32,416},{64,448},{96,480},{128,0},{160,32},{192,64},{224,... | collective-permute-start | bytes 786440 | tf_op jit(solution)/shard_map/ppermute | solution.py:19
  23.5 14.7 %collective-permute-done = bf16[512,256]{1,0:T(8,128)(2,1)S(1)} collective-permute-done((bf16[512,256]{1,0:T(8,128)(2,1)S(1)}, bf16[512,256]{1,0:T(8,128)(2,1)S(1)}, u32[]{:S(2)}, u32[]{:S(2)}) %collective-permute-start) | collective-permute-done | bytes 262176 | tf_op jit(solution)/shard_map/ppermute | solution.py:19
  38.3 16.2 %collective-permute-done.1 = bf16[512,256]{1,0:T(8,128)(2,1)S(1)} collective-permute-done((bf16[512,256]{1,0:T(8,128)(2,1)S(1)}, bf16[512,256]{1,0:T(8,128)(2,1)S(1)}, u32[]{:S(2)}, u32[]{:S(2)}) %collective-permute-start.1) | collective-permute-done | bytes 262176 | tf_op jit(solution)/shard_map/ppermute | solution.py:19
  54.6 4.7 %collective-permute-start.6 = (bf16[3,512,256]{2,1,0:T(8,128)(2,1)S(1)}, bf16[3,512,256]{2,1,0:T(8,128)(2,1)S(1)}, u32[]{:S(2)}, u32[]{:S(2)}) collective-permute-start(bf16[3,512,256]{2,1,0:T(8,128)(2,1)S(1)} %pad_maximum_fusion.refs_0_), channel_id=1, source_target_pairs={{0,96},{32,0},{64,32},{96,64},{128,224},{160,128},{192,160},{224,1... | collective-permute-start | bytes 2359304 | tf_op jit(solution)/shard_map/ppermute | solution.py:19
  61.2 7.1 %collective-permute-start.2 = (bf16[256,256]{1,0:T(8,128)(2,1)S(1)}, bf16[256,256]{1,0:T(8,128)(2,1)S(1)}, u32[]{:S(2)}, u32[]{:S(2)}) collective-permute-start(bf16[256,256]{1,0:T(8,128)(2,1)S(1)} %slice.220), channel_id=1, source_target_pairs={{0,128},{32,160},{64,192},{96,224},{128,256},{160,288},{192,320},{... | collective-permute-start | bytes 393224 | tf_op jit(solution)/shard_map/ppermute | solution.py:19
  71.0 6.0 %collective-permute-done.2 = bf16[256,256]{1,0:T(8,128)(2,1)S(1)} collective-permute-done((bf16[256,256]{1,0:T(8,128)(2,1)S(1)}, bf16[256,256]{1,0:T(8,128)(2,1)S(1)}, u32[]{:S(2)}, u32[]{:S(2)}) %collective-permute-start.2) | collective-permute-done | bytes 131104 | tf_op jit(solution)/shard_map/ppermute | solution.py:19
  77.0 8.1 %collective-permute-done.3 = bf16[256,256]{1,0:T(8,128)(2,1)S(1)} collective-permute-done((bf16[256,256]{1,0:T(8,128)(2,1)S(1)}, bf16[256,256]{1,0:T(8,128)(2,1)S(1)}, u32[]{:S(2)}, u32[]{:S(2)}) %collective-permute-start.3) | collective-permute-done | bytes 131104 | tf_op jit(solution)/shard_map/ppermute | solution.py:19
  85.1 5.0 %collective-permute-start.7 = (bf16[1,512,256]{2,1,0:T(8,128)(2,1)S(1)}, bf16[1,512,256]{2,1,0:T(8,128)(2,1)S(1)}, u32[]{:S(2)}, u32[]{:S(2)}) collective-permute-start(bf16[1,512,256]{2,1,0:T(8,128)(2,1)S(1)} %maximum_bitcast_fusion.refs_1_), channel_id=1, source_target_pairs={{0,96},{32,0},{64,32},{96,64},{128,224},{160,128},{192,160},{224,1... | collective-permute-start | bytes 786440 | tf_op jit(solution)/shard_map/ppermute | solution.py:19
  90.1 4.9 %collective-permute-done.7.refs_5_ = bf16[1,512,256]{2,1,0:T(8,128)(2,1)S(1)} collective-permute-done((bf16[1,512,256]{2,1,0:T(8,128)(2,1)S(1)}, bf16[1,512,256]{2,1,0:T(8,128)(2,1)S(1)}, u32[]{:S(2)}, u32[]{:S(2)}) %collective-permute-start.7) | collective-permute-done | bytes 262176 | tf_op jit(solution)/shard_map/ppermute | solution.py:19
  95.8 5.6 %collective-permute-start.9 = (bf16[2,512,256]{2,1,0:T(8,128)(2,1)}, bf16[2,512,256]{2,1,0:T(8,128)(2,1)S(1)}, u32[]{:S(2)}, u32[]{:S(2)}) collective-permute-start(bf16[2,512,256]{2,1,0:T(8,128)(2,1)} %pad_maximum_fusion.1), channel_id=1, source_target_pairs={{0,96},{32,0},{64,32},{96,64},{128,224},{160,128},{192,160},{224,1... | collective-permute-start | bytes 1572872 | tf_op jit(solution)/shard_map/ppermute | solution.py:19
  110.0 13.3 %collective-permute-done.5.refs_3_ = bf16[1,512,256]{2,1,0:T(8,128)(2,1)} collective-permute-done((bf16[1,512,256]{2,1,0:T(8,128)(2,1)S(1)}, bf16[1,512,256]{2,1,0:T(8,128)(2,1)}, u32[]{:S(2)}, u32[]{:S(2)}) %collective-permute-start.5) | collective-permute-done | bytes 262176 | tf_op jit(solution)/shard_map/ppermute | solution.py:19
  123.3 10.2 %shard_map.110 = (bf16[256,512]{1,0:T(8,128)(2,1)}, bf16[256,256]{1,0:T(8,128)(2,1)S(1)}) custom-call(s32[2]{0:T(128)S(1)} %pad_add_fusion.1.idx_ref, bf16[32,512,256]{2,1,0:T(8,128)(2,1)} %all-gather.2.cloned.1.call-done.x_ref, bf16[3,512,256]{2,1,0:T(8,128)(2,1)S(1)} %pad_maximum_fusion.refs_0_, bf16[1,512,256]{2,1,0:T(8,128)(2,1)S(1)} %maximum_bitcast_fusion.refs_1_, ...), custom_call_target="tpu_custom_call" | custom-call | tf_op jit(solution)/shard_map/pallas_call | solution.py:84
  143.3 6.0 %shard_map.112 = (bf16[256,512]{1,0:T(8,128)(2,1)}, bf16[128,768]{1,0:T(8,128)(2,1)}, f32[16,128]{1,0:T(8,128)}) custom-call(bf16[256,512]{1,0:T(8,128)(2,1)} %get-tuple-element.25.kv_ref, bf16[256,512]{1,0:T(8,128)(2,1)} %copy-done.3, bf16[256,256]{1,0:T(8,128)(2,1)} %copy-done.4, f32[128,768]{1,0:T(8,128)} %get-tuple-element.27.grad_ref, f32[256,8]{1,0:T(8,128)} %pad.5.taps_ref), custom_call_target="tpu_custom_call" | custom-call | tf_op jit(solution)/shard_map/pallas_call | solution.py:339
  156.7 4.6 %collective-permute-start.17 = (bf16[288,512]{1,0:T(8,128)(2,1)S(1)}, bf16[288,512]{1,0:T(8,128)(2,1)S(1)}, u32[]{:S(2)}, u32[]{:S(2)}) collective-permute-start(bf16[288,512]{1,0:T(8,128)(2,1)S(1)} %get-tuple-element.42), channel_id=1, source_target_pairs={{0,32},{32,64},{64,96},{96,0},{128,160},{160,192},{192,224},{224,1... | collective-permute-start | bytes 884744 | tf_op jit(solution)/shard_map/ppermute | solution.py:19
  161.3 8.3 %collective-permute-start.16 = (bf16[288,512]{1,0:T(8,128)(2,1)S(1)}, bf16[288,512]{1,0:T(8,128)(2,1)S(1)}, u32[]{:S(2)}, u32[]{:S(2)}) collective-permute-start(bf16[288,512]{1,0:T(8,128)(2,1)S(1)} %get-tuple-element.40), channel_id=1, source_target_pairs={{0,96},{32,0},{64,32},{96,64},{128,224},{160,128},{192,160},{224,1... | collective-permute-start | bytes 884744 | tf_op jit(solution)/shard_map/ppermute | solution.py:19
  174.7 5.4 %shard_map.114 = (bf16[768,512]{1,0:T(8,128)(2,1)S(1)}, bf16[768,512]{1,0:T(8,128)(2,1)S(1)}, bf16[384,512]{1,0:T(8,128)(2,1)S(1)}, bf16[384,512]{1,0:T(8,128)(2,1)S(1)}, bf16[768,512]{1,0:T(8,128)(2,1)S(1)}) custom-call(s32[2]{0:T(128)S(1)} %pad_add_fusion.1.idx_ref, bf16[32,512,256]{2,1,0:T(8,128)(2,1)} %all-gather.2.cloned.1.call-done.x_ref, ...), custom_call_target="tpu_custom_call" | custom-call | tf_op jit(solution)/shard_map/pallas_call | solution.py:175
  191.3 8.6 %collective-permute-done.14 = bf16[768,512]{1,0:T(8,128)(2,1)S(1)} collective-permute-done((bf16[768,512]{1,0:T(8,128)(2,1)S(1)}, bf16[768,512]{1,0:T(8,128)(2,1)S(1)}, u32[]{:S(2)}, u32[]{:S(2)}) %collective-permute-start.14) | collective-permute-done | bytes 786464 | tf_op jit(solution)/shard_map/ppermute | solution.py:19
  202.6 5.6 %collective-permute-start.20 = (bf16[384,512]{1,0:T(8,128)(2,1)S(1)}, bf16[384,512]{1,0:T(8,128)(2,1)S(1)}, u32[]{:S(2)}, u32[]{:S(2)}) collective-permute-start(bf16[384,512]{1,0:T(8,128)(2,1)S(1)} %add_convert_fusion), channel_id=1, source_target_pairs={{0,96},{32,0},{64,32},{96,64},{128,224},{160,128},{192,160},{224,1... | collective-permute-start | bytes 1179656 | tf_op jit(solution)/shard_map/ppermute | solution.py:19
  208.3 10.6 %collective-permute-start.19 = (bf16[160,512]{1,0:T(8,128)(2,1)S(1)}, bf16[160,512]{1,0:T(8,128)(2,1)S(1)}, u32[]{:S(2)}, u32[]{:S(2)}) collective-permute-start(bf16[160,512]{1,0:T(8,128)(2,1)S(1)} %get-tuple-element.63), channel_id=1, source_target_pairs={{0,128},{32,160},{64,192},{96,224},{128,256},{160,288},{192,320},{... | collective-permute-start | bytes 491528 | tf_op jit(solution)/shard_map/ppermute | solution.py:19
  220.8 7.3 %collective-permute-done.19 = bf16[160,512]{1,0:T(8,128)(2,1)S(1)} collective-permute-done((bf16[160,512]{1,0:T(8,128)(2,1)S(1)}, bf16[160,512]{1,0:T(8,128)(2,1)S(1)}, u32[]{:S(2)}, u32[]{:S(2)}) %collective-permute-start.19) | collective-permute-done | bytes 163872 | tf_op jit(solution)/shard_map/ppermute | solution.py:19
  228.5 8.4 %collective-permute-start.21 = (bf16[288,512]{1,0:T(8,128)(2,1)S(1)}, bf16[288,512]{1,0:T(8,128)(2,1)S(1)}, u32[]{:S(2)}, u32[]{:S(2)}) collective-permute-start(bf16[288,512]{1,0:T(8,128)(2,1)S(1)} %pad_maximum_fusion.2), channel_id=1, source_target_pairs={{0,128},{32,160},{64,192},{96,224},{128,256},{160,288},{192,320},{... | collective-permute-start | bytes 884744 | tf_op jit(solution)/shard_map/ppermute | solution.py:19
  238.9 6.3 %collective-permute-done.21 = bf16[288,512]{1,0:T(8,128)(2,1)S(1)} collective-permute-done((bf16[288,512]{1,0:T(8,128)(2,1)S(1)}, bf16[288,512]{1,0:T(8,128)(2,1)S(1)}, u32[]{:S(2)}, u32[]{:S(2)}) %collective-permute-start.21) | collective-permute-done | bytes 294944 | tf_op jit(solution)/shard_map/ppermute | solution.py:19
  246.0 16.3 %collective-permute-done.24 = bf16[256,512]{1,0:T(8,128)(2,1)S(1)} collective-permute-done((bf16[256,512]{1,0:T(8,128)(2,1)S(1)}, bf16[256,512]{1,0:T(8,128)(2,1)S(1)}, u32[]{:S(2)}, u32[]{:S(2)}) %collective-permute-start.24) | collective-permute-done | bytes 262176 | tf_op jit(solution)/shard_map/ppermute | solution.py:19
  (96 shorter events, 60.1 us)
Async XLA Ops:
  7.2 116.1 %all-gather.2.cloned.1.call-start = ((), (), s32[]{:S(2)}) async-start(), calls=%async_computation | async-start | bytes 8650752 | tf_op jit(solution)/shard_map/all_gather | solution.py:403
  9.8 28.5 %collective-permute-start = (bf16[512,256]{1,0:T(8,128)(2,1)S(1)}, bf16[512,256]{1,0:T(8,128)(2,1)S(1)}, u32[]{:S(2)}, u32[]{:S(2)}) collective-permute-start(bf16[512,256]{1,0:T(8,128)(2,1)S(1)} %constant_dynamic-update-slice_fusion), channel_id=1, source_target_pairs={{0,128},{32,160},{64,192},{96,224},{128,256},{160,288},{192,320},{... | collective-permute-start | bytes 786440 | tf_op jit(solution)/shard_map/ppermute | solution.py:19
  18.9 35.6 %collective-permute-start.1 = (bf16[512,256]{1,0:T(8,128)(2,1)S(1)}, bf16[512,256]{1,0:T(8,128)(2,1)S(1)}, u32[]{:S(2)}, u32[]{:S(2)}) collective-permute-start(bf16[512,256]{1,0:T(8,128)(2,1)S(1)} %constant_dynamic-update-slice_fusion), channel_id=1, source_target_pairs={{0,384},{32,416},{64,448},{96,480},{128,0},{160,32},{192,64},{224,... | collective-permute-start | bytes 786440 | tf_op jit(solution)/shard_map/ppermute | solution.py:19
  54.6 35.5 %collective-permute-start.6 = (bf16[3,512,256]{2,1,0:T(8,128)(2,1)S(1)}, bf16[3,512,256]{2,1,0:T(8,128)(2,1)S(1)}, u32[]{:S(2)}, u32[]{:S(2)}) collective-permute-start(bf16[3,512,256]{2,1,0:T(8,128)(2,1)S(1)} %pad_maximum_fusion.refs_0_), channel_id=1, source_target_pairs={{0,96},{32,0},{64,32},{96,64},{128,224},{160,128},{192,160},{224,1... | collective-permute-start | bytes 2359304 | tf_op jit(solution)/shard_map/ppermute | solution.py:19
  59.3 42.2 %collective-permute-start.4 = (bf16[3,512,256]{2,1,0:T(8,128)(2,1)S(1)}, bf16[3,512,256]{2,1,0:T(8,128)(2,1)S(1)}, u32[]{:S(2)}, u32[]{:S(2)}) collective-permute-start(bf16[3,512,256]{2,1,0:T(8,128)(2,1)S(1)} %pad_maximum_fusion.refs_0_), channel_id=1, source_target_pairs={{0,32},{32,64},{64,96},{96,0},{128,160},{160,192},{192,224},{224,1... | collective-permute-start | bytes 2359304 | tf_op jit(solution)/shard_map/ppermute | solution.py:19
  61.2 15.8 %collective-permute-start.2 = (bf16[256,256]{1,0:T(8,128)(2,1)S(1)}, bf16[256,256]{1,0:T(8,128)(2,1)S(1)}, u32[]{:S(2)}, u32[]{:S(2)}) collective-permute-start(bf16[256,256]{1,0:T(8,128)(2,1)S(1)} %slice.220), channel_id=1, source_target_pairs={{0,128},{32,160},{64,192},{96,224},{128,256},{160,288},{192,320},{... | collective-permute-start | bytes 393224 | tf_op jit(solution)/shard_map/ppermute | solution.py:19
  68.3 16.7 %collective-permute-start.3 = (bf16[256,256]{1,0:T(8,128)(2,1)S(1)}, bf16[256,256]{1,0:T(8,128)(2,1)S(1)}, u32[]{:S(2)}, u32[]{:S(2)}) collective-permute-start(bf16[256,256]{1,0:T(8,128)(2,1)S(1)} %slice.221), channel_id=1, source_target_pairs={{0,384},{32,416},{64,448},{96,480},{128,0},{160,32},{192,64},{224,... | collective-permute-start | bytes 393224 | tf_op jit(solution)/shard_map/ppermute | solution.py:19
  85.1 9.9 %collective-permute-start.7 = (bf16[1,512,256]{2,1,0:T(8,128)(2,1)S(1)}, bf16[1,512,256]{2,1,0:T(8,128)(2,1)S(1)}, u32[]{:S(2)}, u32[]{:S(2)}) collective-permute-start(bf16[1,512,256]{2,1,0:T(8,128)(2,1)S(1)} %maximum_bitcast_fusion.refs_1_), channel_id=1, source_target_pairs={{0,96},{32,0},{64,32},{96,64},{128,224},{160,128},{192,160},{224,1... | collective-permute-start | bytes 786440 | tf_op jit(solution)/shard_map/ppermute | solution.py:19
  95.8 27.4 %collective-permute-start.9 = (bf16[2,512,256]{2,1,0:T(8,128)(2,1)}, bf16[2,512,256]{2,1,0:T(8,128)(2,1)S(1)}, u32[]{:S(2)}, u32[]{:S(2)}) collective-permute-start(bf16[2,512,256]{2,1,0:T(8,128)(2,1)} %pad_maximum_fusion.1), channel_id=1, source_target_pairs={{0,96},{32,0},{64,32},{96,64},{128,224},{160,128},{192,160},{224,1... | collective-permute-start | bytes 1572872 | tf_op jit(solution)/shard_map/ppermute | solution.py:19
  102.3 20.9 %collective-permute-start.8 = (bf16[2,512,256]{2,1,0:T(8,128)(2,1)}, bf16[2,512,256]{2,1,0:T(8,128)(2,1)}, u32[]{:S(2)}, u32[]{:S(2)}) collective-permute-start(bf16[2,512,256]{2,1,0:T(8,128)(2,1)} %slice.222), channel_id=1, source_target_pairs={{0,32},{32,64},{64,96},{96,0},{128,160},{160,192},{192,224},{224,1... | collective-permute-start | bytes 1572872 | tf_op jit(solution)/shard_map/ppermute | solution.py:19
  104.2 19.0 %collective-permute-start.5 = (bf16[1,512,256]{2,1,0:T(8,128)(2,1)S(1)}, bf16[1,512,256]{2,1,0:T(8,128)(2,1)}, u32[]{:S(2)}, u32[]{:S(2)}) collective-permute-start(bf16[1,512,256]{2,1,0:T(8,128)(2,1)S(1)} %maximum_bitcast_fusion.refs_1_), channel_id=1, source_target_pairs={{0,32},{32,64},{64,96},{96,0},{128,160},{160,192},{192,224},{224,1... | collective-permute-start | bytes 786440 | tf_op jit(solution)/shard_map/ppermute | solution.py:19
  107.7 32.5 %collective-permute-start.12 = (bf16[2,144,128]{2,1,0:T(8,128)(2,1)}, bf16[2,144,128]{2,1,0:T(8,128)(2,1)}, u32[]{:S(2)}, u32[]{:S(2)}) collective-permute-start(bf16[2,144,128]{2,1,0:T(8,128)(2,1)} %slice.174), channel_id=1, source_target_pairs={{32,0},{64,32},{96,64},{128,96},{160,128},{192,160},{224,192},{256... | collective-permute-start | bytes 221192 | tf_op jit(solution)/shard_map/ppermute | solution.py:24
  156.7 15.9 %collective-permute-start.17 = (bf16[288,512]{1,0:T(8,128)(2,1)S(1)}, bf16[288,512]{1,0:T(8,128)(2,1)S(1)}, u32[]{:S(2)}, u32[]{:S(2)}) collective-permute-start(bf16[288,512]{1,0:T(8,128)(2,1)S(1)} %get-tuple-element.42), channel_id=1, source_target_pairs={{0,32},{32,64},{64,96},{96,0},{128,160},{160,192},{192,224},{224,1... | collective-permute-start | bytes 884744 | tf_op jit(solution)/shard_map/ppermute | solution.py:19
  161.3 25.9 %collective-permute-start.16 = (bf16[288,512]{1,0:T(8,128)(2,1)S(1)}, bf16[288,512]{1,0:T(8,128)(2,1)S(1)}, u32[]{:S(2)}, u32[]{:S(2)}) collective-permute-start(bf16[288,512]{1,0:T(8,128)(2,1)S(1)} %get-tuple-element.40), channel_id=1, source_target_pairs={{0,96},{32,0},{64,32},{96,64},{128,224},{160,128},{192,160},{224,1... | collective-permute-start | bytes 884744 | tf_op jit(solution)/shard_map/ppermute | solution.py:19
  172.6 14.6 %collective-permute-start.18 = (bf16[160,512]{1,0:T(8,128)(2,1)S(1)}, bf16[160,512]{1,0:T(8,128)(2,1)S(1)}, u32[]{:S(2)}, u32[]{:S(2)}) collective-permute-start(bf16[160,512]{1,0:T(8,128)(2,1)S(1)} %pad_maximum_fusion.4), channel_id=1, source_target_pairs={{0,32},{32,64},{64,96},{96,0},{128,160},{160,192},{192,224},{224,1... | collective-permute-start | bytes 491528 | tf_op jit(solution)/shard_map/ppermute | solution.py:19
  180.1 19.8 %collective-permute-start.14 = (bf16[768,512]{1,0:T(8,128)(2,1)S(1)}, bf16[768,512]{1,0:T(8,128)(2,1)S(1)}, u32[]{:S(2)}, u32[]{:S(2)}) collective-permute-start(bf16[768,512]{1,0:T(8,128)(2,1)S(1)} %get-tuple-element.37), channel_id=1, source_target_pairs={{0,32},{32,64},{64,96},{96,0},{128,160},{160,192},{192,224},{224,1... | collective-permute-start | bytes 2359304 | tf_op jit(solution)/shard_map/ppermute | solution.py:19
  182.7 19.7 %collective-permute-start.13 = (bf16[768,512]{1,0:T(8,128)(2,1)S(1)}, bf16[768,512]{1,0:T(8,128)(2,1)S(1)}, u32[]{:S(2)}, u32[]{:S(2)}) collective-permute-start(bf16[768,512]{1,0:T(8,128)(2,1)S(1)} %get-tuple-element.35), channel_id=1, source_target_pairs={{0,96},{32,0},{64,32},{96,64},{128,224},{160,128},{192,160},{224,1... | collective-permute-start | bytes 2359304 | tf_op jit(solution)/shard_map/ppermute | solution.py:19
  187.3 20.9 %collective-permute-start.22 = (bf16[128,512]{1,0:T(8,128)(2,1)S(1)}, bf16[128,512]{1,0:T(8,128)(2,1)S(1)}, u32[]{:S(2)}, u32[]{:S(2)}) collective-permute-start(bf16[128,512]{1,0:T(8,128)(2,1)S(1)} %get-tuple-element.62), channel_id=1, source_target_pairs={{0,96},{32,0},{64,32},{96,64},{128,224},{160,128},{192,160},{224,1... | collective-permute-start | bytes 393224 | tf_op jit(solution)/shard_map/ppermute | solution.py:19
  200.0 28.1 %collective-permute-start.15 = (bf16[384,512]{1,0:T(8,128)(2,1)S(1)}, bf16[384,512]{1,0:T(8,128)(2,1)S(1)}, u32[]{:S(2)}, u32[]{:S(2)}) collective-permute-start(bf16[384,512]{1,0:T(8,128)(2,1)S(1)} %add_convert_fusion.1), channel_id=1, source_target_pairs={{0,32},{32,64},{64,96},{96,0},{128,160},{160,192},{192,224},{224,1... | collective-permute-start | bytes 1179656 | tf_op jit(solution)/shard_map/ppermute | solution.py:19
  202.6 25.5 %collective-permute-start.20 = (bf16[384,512]{1,0:T(8,128)(2,1)S(1)}, bf16[384,512]{1,0:T(8,128)(2,1)S(1)}, u32[]{:S(2)}, u32[]{:S(2)}) collective-permute-start(bf16[384,512]{1,0:T(8,128)(2,1)S(1)} %add_convert_fusion), channel_id=1, source_target_pairs={{0,96},{32,0},{64,32},{96,64},{128,224},{160,128},{192,160},{224,1... | collective-permute-start | bytes 1179656 | tf_op jit(solution)/shard_map/ppermute | solution.py:19
  208.3 19.8 %collective-permute-start.19 = (bf16[160,512]{1,0:T(8,128)(2,1)S(1)}, bf16[160,512]{1,0:T(8,128)(2,1)S(1)}, u32[]{:S(2)}, u32[]{:S(2)}) collective-permute-start(bf16[160,512]{1,0:T(8,128)(2,1)S(1)} %get-tuple-element.63), channel_id=1, source_target_pairs={{0,128},{32,160},{64,192},{96,224},{128,256},{160,288},{192,320},{... | collective-permute-start | bytes 491528 | tf_op jit(solution)/shard_map/ppermute | solution.py:19
  218.9 18.0 %collective-permute-start.23 = (bf16[160,512]{1,0:T(8,128)(2,1)S(1)}, bf16[160,512]{1,0:T(8,128)(2,1)S(1)}, u32[]{:S(2)}, u32[]{:S(2)}) collective-permute-start(bf16[160,512]{1,0:T(8,128)(2,1)S(1)} %get-tuple-element.64), channel_id=1, source_target_pairs={{0,384},{32,416},{64,448},{96,480},{128,0},{160,32},{192,64},{224,... | collective-permute-start | bytes 491528 | tf_op jit(solution)/shard_map/ppermute | solution.py:19
  228.5 16.7 %collective-permute-start.21 = (bf16[288,512]{1,0:T(8,128)(2,1)S(1)}, bf16[288,512]{1,0:T(8,128)(2,1)S(1)}, u32[]{:S(2)}, u32[]{:S(2)}) collective-permute-start(bf16[288,512]{1,0:T(8,128)(2,1)S(1)} %pad_maximum_fusion.2), channel_id=1, source_target_pairs={{0,128},{32,160},{64,192},{96,224},{128,256},{160,288},{192,320},{... | collective-permute-start | bytes 884744 | tf_op jit(solution)/shard_map/ppermute | solution.py:19
  237.0 25.3 %collective-permute-start.24 = (bf16[256,512]{1,0:T(8,128)(2,1)S(1)}, bf16[256,512]{1,0:T(8,128)(2,1)S(1)}, u32[]{:S(2)}, u32[]{:S(2)}) collective-permute-start(bf16[256,512]{1,0:T(8,128)(2,1)S(1)} %pad_maximum_fusion.3), channel_id=1, source_target_pairs={{0,384},{32,416},{64,448},{96,480},{128,0},{160,32},{192,64},{224,... | collective-permute-start | bytes 786440 | tf_op jit(solution)/shard_map/ppermute | solution.py:19
  (8 other events, 138.8 us)
Sparse Core Ops, SparseCore 0:
  10.1 100.8 all-gather.1
where the time goes:
time: 272 us; the launch traced here: 271 us
  waiting for transfers between devices  106 us (39%)
  starting transfers between devices  105 us (39%)
  Pallas kernels  29.7 us (11%)
  between operations  14.6 us (5%)
  local copies, waits for them, and re-layouts  12 us (4%)
  other arithmetic  4.56 us (2%)
    ppermute x22, waiting for transfers between devices, dp_move(): return lax.ppermute(value, 'dp', pairs)  105 us
    ppermute x22, starting transfers between devices, dp_move(): return lax.ppermute(value, 'dp', pairs)  101 us
    pallas_call x1, Pallas kernels, forward_matmul(): pl.pallas_call(forward_kernel, out_shape=[jax.ShapeDtypeStruct((width, ro...  10.2 us
    pallas_call x2, Pallas kernels, backward_matmul(): pl.pallas_call(functools.partial(backward_kernel, rels), out_shape=[sent,...  8.21 us
    unnamed x17, local copies, waits for them, and re-layouts  6.28 us
    pallas_call x1, Pallas kernels, middle_terms(): pl.pallas_call(middle_kernel, out_shape=[jax.ShapeDtypeStruct((256, 512),...  6.02 us
  transfers between devices with their start and end apart: 26, of which 12 were waited for; matrix products, arithmetic and copies ran while one was open for 4% of the time, Pallas kernels for 7%

commit v1 on v0

--- a/solution.py
+++ b/solution.py
@@ -45,9 +45,10 @@
 ZH_REL = (0, 3, 1, 2)
 
 
-def forward_kernel(idx_ref, x_ref, *refs):
-    w_refs, (out_ref, head_ref, x_buf, w_buf, x_sem, w_sem) = refs[:8], refs[8:]
+def forward_kernel(idx_ref, x_ref, taps_ref, *refs):
+    w_refs, (out_ref, prev_ref, head_ref, x_buf, w_buf, x_sem, w_sem) = refs[:8], refs[8:]
     blocks, rows, depth = x_ref.shape
+    width, half = w_buf.shape[2], rows // 2
     for block in range(blocks):
         pltpu.make_async_copy(
             x_ref.at[block], x_buf.at[:, block * depth : (block + 1) * depth], x_sem.at[block]
@@ -57,7 +58,7 @@
         for k in range(ref.shape[0]):
             slot = lax.rem(idx_ref[0] + ZH_REL[first + k], 4) * 4 + lax.rem(idx_ref[1] + rel, 4)
             pltpu.make_async_copy(ref.at[k], w_buf.at[slot], w_sem.at[slot]).start()
-    total = jnp.zeros((rows, w_buf.shape[2]), F32)
+    totals = [jnp.zeros((half, width), F32) for _ in range(2)]
     for part in range(4):
         for block in range(8 * part, 8 * part + 8):
             pltpu.make_async_copy(
@@ -65,34 +66,49 @@
             ).wait()
         for slot in range(4 * part, 4 * part + 4):
             pltpu.make_async_copy(w_refs[0].at[0], w_buf.at[slot], w_sem.at[slot]).wait()
-        weights = w_buf[4 * part : 4 * part + 4].reshape(8 * depth, w_buf.shape[2])
-        total = total + jnp.dot(
-            x_buf[:, 8 * part * depth : 8 * (part + 1) * depth],
-            weights,
-            preferred_element_type=F32,
-        )
-    turned = total.T.astype(BF)
-    out_ref[...] = turned
-    half = turned.shape[1] // 2
-    head_ref[:, :128] = turned[:, :128]
-    head_ref[:, 128:] = turned[:, half : half + 128]
-
-
-def forward_matmul(idx, features, panels):
+        weights = w_buf[4 * part : 4 * part + 4].reshape(8 * depth, width)
+        for s in range(2):
+            totals[s] = totals[s] + jnp.dot(
+                x_buf[s * half : (s + 1) * half, 8 * part * depth : 8 * (part + 1) * depth],
+                weights,
+                preferred_element_type=F32,
+            )
+    head_ref[...] = jnp.concatenate([total[:8] for total in totals]).astype(BF)
+    prev_ref[128:] = jnp.concatenate([total[half - 8 :] for total in totals]).astype(BF)
+    for s in range(2):
+        turned = totals[s].T.astype(BF)
+        out_ref[:, s * half : (s + 1) * half] = turned
+        smooth = []
+        for b in range(2):
+            branch = slice(128 * b, 128 * b + 128)
+            smooth.append(short_smooth(turned[branch].astype(F32), taps_ref, branch)[:, half - 128 :])
+        prev_ref[:128, s * 128 : (s + 1) * 128] = (smooth[0] * smooth[1]).astype(BF)
+
+
+def short_smooth(ext, taps_ref, rows):
+    total = taps_ref[rows, 0:1] * ext
+    for j in range(1, 7):
+        total = total + taps_ref[rows, j : j + 1] * pltpu.roll(ext, j, 1)
+    return total
+
+
+def forward_matmul(idx, features, taps, panels):
     blocks, rows, depth = features.shape
     width = panels[0].shape[2]
     return pl.pallas_call(
         forward_kernel,
         out_shape=[
             jax.ShapeDtypeStruct((width, rows), BF),
-            jax.ShapeDtypeStruct((width, 256), BF),
+            jax.ShapeDtypeStruct((144, width), BF),
+            jax.ShapeDtypeStruct((16, width), BF),
         ],
         in_specs=[
             pl.BlockSpec(memory_space=pltpu.SMEM),
             pl.BlockSpec(memory_space=pltpu.HBM),
+            pl.BlockSpec(memory_space=pltpu.VMEM),
         ]
         + [pl.BlockSpec(memory_space=pl.ANY)] * 8,
-        out_specs=[pl.BlockSpec(memory_space=pltpu.VMEM)] * 2,
+        out_specs=[pl.BlockSpec(memory_space=pltpu.VMEM)] * 3,
         scratch_shapes=[
             pltpu.VMEM((rows, blocks * depth), BF),
             pltpu.VMEM((blocks // 2, 2 * depth, width), BF),
@@ -100,7 +116,7 @@
             pltpu.SemaphoreType.DMA((blocks // 2,)),
         ],
         compiler_params=pltpu.CompilerParams(vmem_limit_bytes=40 << 20),
-    )(idx, features, *panels)
+    )(idx, features, taps, *panels)
 
 
 GROUPS = ((2,), (1, 3, 0))
@@ -298,26 +314,29 @@
     lanes = lax.broadcasted_iota(jnp.int32, (128, 128), 1)
     sums = jnp.zeros((128, 128), F32)
     partial = [[None] * 7 for _ in range(2)]
+    zeros = jnp.zeros((112, 256), F32)
+    before = jnp.concatenate([prev_ref[128:].astype(F32), zeros]).T
+    after = jnp.concatenate([head_ref[...].astype(F32), zeros]).T
     for s in range(2):
         smooth = []
         for b in range(2):
             rows = slice(128 * b, 128 * b + 128)
             ext = jnp.concatenate(
                 [
-                    prev_ref[rows, s * 256 : (s + 1) * 256],
-                    kv_ref[rows, s * 256 : (s + 1) * 256],
-                    head_ref[rows, s * 128 : (s + 1) * 128],
+                    pltpu.roll(before[rows], 120 - 8 * s, 1),
+                    kv_ref[rows, s * 256 : (s + 1) * 256].astype(F32),
+                    after[rows] if s == 0 else pltpu.roll(after[rows], 120, 1),
                 ],
                 axis=1,
-            ).astype(F32)
-            total = taps_ref[rows, 0:1] * ext
-            for j in range(1, 7):
-                total = total + taps_ref[rows, j : j + 1] * pltpu.roll(ext, j, 1)
-            smooth.append(total[:, 128:])
-        prod_ref[:, s * 384 : (s + 1) * 384] = (smooth[0][:, :384] * smooth[1][:, :384]).astype(BF)
+            )
+            smooth.append(short_smooth(ext, taps_ref, rows)[:, 128:])
+        prod_ref[:, s * 384 : s * 384 + 128] = prev_ref[:128, s * 128 : (s + 1) * 128]
+        prod_ref[:, s * 384 + 128 : (s + 1) * 384] = (
+            smooth[0][:, :256] * smooth[1][:, :256]
+        ).astype(BF)
         for b in range(2):
             rows = slice(128 * b, 128 * b + 128)
-            slope = grad_ref[:, s * 384 : (s + 1) * 384] * smooth[1 - b][:, 128:512]
+            slope = grad_ref[:, s * 384 : (s + 1) * 384] * smooth[1 - b]
             own = kv_ref[rows, s * 256 : (s + 1) * 256].astype(F32)
             act = jnp.zeros((128, 256), F32)
             for j in range(7):
@@ -334,8 +353,7 @@
     sums_ref[...] = sums.T[0:16]
 
 
-def middle_terms(kv, prev, head, grad, short_filters):
-    taps = jnp.pad(short_filters.reshape(256, 7), ((0, 0), (0, 1)))
+def middle_terms(kv, prev, head, grad, taps):
     return pl.pallas_call(
         middle_kernel,
         out_shape=[
@@ -406,10 +424,11 @@
     after = shifted(cotangent[:, :144], -1)
     up, product_grad, bands = cotangent_terms(meta, cotangent, after, medium_filters)
 
-    kv, head = forward_matmul(idx, features, panels)
-    prev = shifted(kv, 1)
+    taps = jnp.pad(short_filters.reshape(256, 7), ((0, 0), (0, 1)))
+    kv, prev, head = forward_matmul(idx, features, taps, panels)
+    prev = shifted(prev, 1)
     head = shifted(head, -1)
-    outgoing, product, sums = middle_terms(kv, prev, head, product_grad, short_filters)
+    outgoing, product, sums = middle_terms(kv, prev, head, product_grad, taps)
 
     mixed, small = response_terms(meta, product, up, bands, sums)
     key_grad, value_grad, small = reduce_grads(idx, features, outgoing, small)

time: 272 us -> 265 us (0.974)
  the two profiles are of different devices: /device:TPU:32 before, /device:TPU:22 now
where the time goes in v1:
time: 265 us; the launch traced here: 264 us
  starting transfers between devices  105 us (40%)
  waiting for transfers between devices  97.2 us (37%)
  Pallas kernels  28.6 us (11%)
  between operations  14.6 us (6%)
  local copies, waits for them, and re-layouts  13.5 us (5%)
  other arithmetic  5.23 us (2%)
    ppermute x22, starting transfers between devices, dp_move(): return lax.ppermute(value, 'dp', pairs)  93.6 us
    ppermute x22, waiting for transfers between devices, dp_move(): return lax.ppermute(value, 'dp', pairs)  91.2 us
    ppermute x3, starting transfers between devices, shifted(): lax.ppermute(value, 'dp', [(i, i + steps) for i in range(first, last)])  11.1 us
    pallas_call x1, Pallas kernels, forward_matmul(): pl.pallas_call(forward_kernel, out_shape=[jax.ShapeDtypeStruct((width, ro...  8.86 us
    pallas_call x2, Pallas kernels, backward_matmul(): pl.pallas_call(functools.partial(backward_kernel, rels), out_shape=[sent,...  8.21 us
    unnamed x21, local copies, waits for them, and re-layouts  7.53 us
    pallas_call x1, Pallas kernels, middle_terms(): pl.pallas_call(middle_kernel, out_shape=[jax.ShapeDtypeStruct((256, 512),...  6.24 us
    ppermute x3, waiting for transfers between devices, shifted(): lax.ppermute(value, 'dp', [(i, i + steps) for i in range(first, last)])  5.34 us
  transfers between devices with their start and end apart: 26, of which 13 were waited for; matrix products, arithmetic and copies ran while one was open for 5% of the time, Pallas kernels for 6%

profile of v1, /device:TPU:22, one launch (start us, length us, event | category | flops | bytes accessed | tf_op | source)
XLA Modules:
  0.0 263.9 jit_solution(17291322255892850600)
XLA Ops:
  9.8 9.1 %collective-permute-start = (bf16[512,256]{1,0:T(8,128)(2,1)S(1)}, bf16[512,256]{1,0:T(8,128)(2,1)S(1)}, u32[]{:S(2)}, u32[]{:S(2)}) collective-permute-start(bf16[512,256]{1,0:T(8,128)(2,1)S(1)} %constant_dynamic-update-slice_fusion), channel_id=1, source_target_pairs={{0,128},{32,160},{64,192},{96,224},{128,256},{160,288},{192,320},{... | collective-permute-start | bytes 786440 | tf_op jit(solution)/shard_map/ppermute | solution.py:19
  18.9 5.6 %collective-permute-start.1 = (bf16[512,256]{1,0:T(8,128)(2,1)S(1)}, bf16[512,256]{1,0:T(8,128)(2,1)S(1)}, u32[]{:S(2)}, u32[]{:S(2)}) collective-permute-start(bf16[512,256]{1,0:T(8,128)(2,1)S(1)} %constant_dynamic-update-slice_fusion), channel_id=1, source_target_pairs={{0,384},{32,416},{64,448},{96,480},{128,0},{160,32},{192,64},{224,... | collective-permute-start | bytes 786440 | tf_op jit(solution)/shard_map/ppermute | solution.py:19
  24.4 7.6 %collective-permute-done = bf16[512,256]{1,0:T(8,128)(2,1)S(1)} collective-permute-done((bf16[512,256]{1,0:T(8,128)(2,1)S(1)}, bf16[512,256]{1,0:T(8,128)(2,1)S(1)}, u32[]{:S(2)}, u32[]{:S(2)}) %collective-permute-start) | collective-permute-done | bytes 262176 | tf_op jit(solution)/shard_map/ppermute | solution.py:19
  32.1 18.8 %collective-permute-done.1 = bf16[512,256]{1,0:T(8,128)(2,1)S(1)} collective-permute-done((bf16[512,256]{1,0:T(8,128)(2,1)S(1)}, bf16[512,256]{1,0:T(8,128)(2,1)S(1)}, u32[]{:S(2)}, u32[]{:S(2)}) %collective-permute-start.1) | collective-permute-done | bytes 262176 | tf_op jit(solution)/shard_map/ppermute | solution.py:19
  53.8 4.3 %collective-permute-start.4 = (bf16[3,512,256]{2,1,0:T(8,128)(2,1)S(1)}, bf16[3,512,256]{2,1,0:T(8,128)(2,1)S(1)}, u32[]{:S(2)}, u32[]{:S(2)}) collective-permute-start(bf16[3,512,256]{2,1,0:T(8,128)(2,1)S(1)} %pad_maximum_fusion.refs_0_), channel_id=1, source_target_pairs={{0,32},{32,64},{64,96},{96,0},{128,160},{160,192},{192,224},{224,1... | collective-permute-start | bytes 2359304 | tf_op jit(solution)/shard_map/ppermute | solution.py:19
  58.1 7.5 %collective-permute-start.2 = (bf16[256,256]{1,0:T(8,128)(2,1)S(1)}, bf16[256,256]{1,0:T(8,128)(2,1)S(1)}, u32[]{:S(2)}, u32[]{:S(2)}) collective-permute-start(bf16[256,256]{1,0:T(8,128)(2,1)S(1)} %slice.220), channel_id=1, source_target_pairs={{0,128},{32,160},{64,192},{96,224},{128,256},{160,288},{192,320},{... | collective-permute-start | bytes 393224 | tf_op jit(solution)/shard_map/ppermute | solution.py:19
  67.9 4.7 %collective-permute-done.2 = bf16[256,256]{1,0:T(8,128)(2,1)S(1)} collective-permute-done((bf16[256,256]{1,0:T(8,128)(2,1)S(1)}, bf16[256,256]{1,0:T(8,128)(2,1)S(1)}, u32[]{:S(2)}, u32[]{:S(2)}) %collective-permute-start.2) | collective-permute-done | bytes 131104 | tf_op jit(solution)/shard_map/ppermute | solution.py:19
  72.6 6.1 %collective-permute-done.3 = bf16[256,256]{1,0:T(8,128)(2,1)S(1)} collective-permute-done((bf16[256,256]{1,0:T(8,128)(2,1)S(1)}, bf16[256,256]{1,0:T(8,128)(2,1)S(1)}, u32[]{:S(2)}, u32[]{:S(2)}) %collective-permute-start.3) | collective-permute-done | bytes 131104 | tf_op jit(solution)/shard_map/ppermute | solution.py:19
  80.7 9.4 %collective-permute-done.7.refs_5_ = bf16[1,512,256]{2,1,0:T(8,128)(2,1)S(1)} collective-permute-done((bf16[1,512,256]{2,1,0:T(8,128)(2,1)S(1)}, bf16[1,512,256]{2,1,0:T(8,128)(2,1)S(1)}, u32[]{:S(2)}, u32[]{:S(2)}) %collective-permute-start.7) | collective-permute-done | bytes 262176 | tf_op jit(solution)/shard_map/ppermute | solution.py:19
  93.7 5.1 %collective-permute-start.8 = (bf16[2,512,256]{2,1,0:T(8,128)(2,1)}, bf16[2,512,256]{2,1,0:T(8,128)(2,1)}, u32[]{:S(2)}, u32[]{:S(2)}) collective-permute-start(bf16[2,512,256]{2,1,0:T(8,128)(2,1)} %slice.222), channel_id=1, source_target_pairs={{0,32},{32,64},{64,96},{96,0},{128,160},{160,192},{192,224},{224,1... | collective-permute-start | bytes 1572872 | tf_op jit(solution)/shard_map/ppermute | solution.py:19
  109.0 5.9 %collective-permute-done.5.refs_3_ = bf16[1,512,256]{2,1,0:T(8,128)(2,1)} collective-permute-done((bf16[1,512,256]{2,1,0:T(8,128)(2,1)S(1)}, bf16[1,512,256]{2,1,0:T(8,128)(2,1)}, u32[]{:S(2)}, u32[]{:S(2)}) %collective-permute-start.5) | collective-permute-done | bytes 262176 | tf_op jit(solution)/shard_map/ppermute | solution.py:19
  114.9 8.9 %shard_map.110 = (bf16[256,512]{1,0:T(8,128)(2,1)S(1)}, bf16[144,256]{1,0:T(8,128)(2,1)}, bf16[16,256]{1,0:T(8,128)(2,1)S(1)}) custom-call(s32[2]{0:T(128)S(1)} %pad_add_fusion.1.idx_ref, bf16[32,512,256]{2,1,0:T(8,128)(2,1)} %all-gather.2.cloned.1.call-done.x_ref, f32[256,8]{1,0:T(8,128)S(1)} %pad.5.taps_ref, ...), custom_call_target="tpu_custom_call" | custom-call | tf_op jit(solution)/shard_map/pallas_call | solution.py:98
  124.4 7.3 %collective-permute-start.10 = (bf16[144,256]{1,0:T(8,128)(2,1)}, bf16[144,256]{1,0:T(8,128)(2,1)S(1)}, u32[]{:S(2)}, u32[]{:S(2)}) collective-permute-start(bf16[144,256]{1,0:T(8,128)(2,1)} %get-tuple-element.27), channel_id=1, source_target_pairs={{0,32},{32,64},{64,96},{96,128},{128,160},{160,192},{192,224},{224... | collective-permute-start | bytes 221192 | tf_op jit(solution)/shard_map/ppermute | solution.py:24
  138.0 5.3 %collective-permute-done.11.head_ref = bf16[16,256]{1,0:T(8,128)(2,1)S(1)} collective-permute-done((bf16[16,256]{1,0:T(8,128)(2,1)S(1)}, bf16[16,256]{1,0:T(8,128)(2,1)S(1)}, u32[]{:S(2)}, u32[]{:S(2)}) %collective-permute-start.11) | collective-permute-done | bytes 8224 | tf_op jit(solution)/shard_map/ppermute | solution.py:24
  143.9 6.2 %shard_map.112 = (bf16[256,512]{1,0:T(8,128)(2,1)}, bf16[128,768]{1,0:T(8,128)(2,1)}, f32[16,128]{1,0:T(8,128)}) custom-call(bf16[256,512]{1,0:T(8,128)(2,1)} %copy-done.2, bf16[144,256]{1,0:T(8,128)(2,1)} %copy-done.5, bf16[16,256]{1,0:T(8,128)(2,1)} %copy-done.7, f32[128,768]{1,0:T(8,128)} %get-tuple-element.29.grad_ref, f32[256,8]{1,0:T(8,128)} %copy-done), custom_call_target="tpu_custom_call" | custom-call | tf_op jit(solution)/shard_map/pallas_call | solution.py:357
  159.5 3.9 %collective-permute-start.16 = (bf16[288,512]{1,0:T(8,128)(2,1)S(1)}, bf16[288,512]{1,0:T(8,128)(2,1)S(1)}, u32[]{:S(2)}, u32[]{:S(2)}) collective-permute-start(bf16[288,512]{1,0:T(8,128)(2,1)S(1)} %get-tuple-element.42), channel_id=1, source_target_pairs={{0,96},{32,0},{64,32},{96,64},{128,224},{160,128},{192,160},{224,1... | collective-permute-start | bytes 884744 | tf_op jit(solution)/shard_map/ppermute | solution.py:19
  169.5 5.4 %shard_map.114 = (bf16[768,512]{1,0:T(8,128)(2,1)S(1)}, bf16[768,512]{1,0:T(8,128)(2,1)S(1)}, bf16[384,512]{1,0:T(8,128)(2,1)S(1)}, bf16[384,512]{1,0:T(8,128)(2,1)S(1)}, bf16[768,512]{1,0:T(8,128)(2,1)S(1)}) custom-call(s32[2]{0:T(128)S(1)} %pad_add_fusion.1.idx_ref, bf16[32,512,256]{2,1,0:T(8,128)(2,1)} %all-gather.2.cloned.1.call-done.x_ref, ...), custom_call_target="tpu_custom_call" | custom-call | tf_op jit(solution)/shard_map/pallas_call | solution.py:191
  184.1 8.4 %collective-permute-done.14 = bf16[768,512]{1,0:T(8,128)(2,1)S(1)} collective-permute-done((bf16[768,512]{1,0:T(8,128)(2,1)S(1)}, bf16[768,512]{1,0:T(8,128)(2,1)S(1)}, u32[]{:S(2)}, u32[]{:S(2)}) %collective-permute-start.14) | collective-permute-done | bytes 786464 | tf_op jit(solution)/shard_map/ppermute | solution.py:19
  201.0 4.0 %collective-permute-start.19 = (bf16[160,512]{1,0:T(8,128)(2,1)S(1)}, bf16[160,512]{1,0:T(8,128)(2,1)S(1)}, u32[]{:S(2)}, u32[]{:S(2)}) collective-permute-start(bf16[160,512]{1,0:T(8,128)(2,1)S(1)} %get-tuple-element.65), channel_id=1, source_target_pairs={{0,128},{32,160},{64,192},{96,224},{128,256},{160,288},{192,320},{... | collective-permute-start | bytes 491528 | tf_op jit(solution)/shard_map/ppermute | solution.py:19
  204.9 5.8 %collective-permute-start.23 = (bf16[160,512]{1,0:T(8,128)(2,1)S(1)}, bf16[160,512]{1,0:T(8,128)(2,1)S(1)}, u32[]{:S(2)}, u32[]{:S(2)}) collective-permute-start(bf16[160,512]{1,0:T(8,128)(2,1)S(1)} %get-tuple-element.66), channel_id=1, source_target_pairs={{0,384},{32,416},{64,448},{96,480},{128,0},{160,32},{192,64},{224,... | collective-permute-start | bytes 491528 | tf_op jit(solution)/shard_map/ppermute | solution.py:19
  210.7 13.1 %collective-permute-done.19 = bf16[160,512]{1,0:T(8,128)(2,1)S(1)} collective-permute-done((bf16[160,512]{1,0:T(8,128)(2,1)S(1)}, bf16[160,512]{1,0:T(8,128)(2,1)S(1)}, u32[]{:S(2)}, u32[]{:S(2)}) %collective-permute-start.19) | collective-permute-done | bytes 163872 | tf_op jit(solution)/shard_map/ppermute | solution.py:19
  224.3 15.9 %collective-permute-start.21 = (bf16[288,512]{1,0:T(8,128)(2,1)S(1)}, bf16[288,512]{1,0:T(8,128)(2,1)S(1)}, u32[]{:S(2)}, u32[]{:S(2)}) collective-permute-start(bf16[288,512]{1,0:T(8,128)(2,1)S(1)} %pad_maximum_fusion.2), channel_id=1, source_target_pairs={{0,128},{32,160},{64,192},{96,224},{128,256},{160,288},{192,320},{... | collective-permute-start | bytes 884744 | tf_op jit(solution)/shard_map/ppermute | solution.py:19
  242.2 4.2 %collective-permute-done.21 = bf16[288,512]{1,0:T(8,128)(2,1)S(1)} collective-permute-done((bf16[288,512]{1,0:T(8,128)(2,1)S(1)}, bf16[288,512]{1,0:T(8,128)(2,1)S(1)}, u32[]{:S(2)}, u32[]{:S(2)}) %collective-permute-start.21) | collective-permute-done | bytes 294944 | tf_op jit(solution)/shard_map/ppermute | solution.py:19
  247.2 7.5 %collective-permute-done.24 = bf16[256,512]{1,0:T(8,128)(2,1)S(1)} collective-permute-done((bf16[256,512]{1,0:T(8,128)(2,1)S(1)}, bf16[256,512]{1,0:T(8,128)(2,1)S(1)}, u32[]{:S(2)}, u32[]{:S(2)}) %collective-permute-start.24) | collective-permute-done | bytes 262176 | tf_op jit(solution)/shard_map/ppermute | solution.py:19
  (100 shorter events, 69.3 us)
Async XLA Ops:
  7.2 107.7 %all-gather.2.cloned.1.call-start = ((), (), s32[]{:S(2)}) async-start(), calls=%async_computation | async-start | bytes 8650752 | tf_op jit(solution)/shard_map/all_gather | solution.py:421
  9.8 22.3 %collective-permute-start = (bf16[512,256]{1,0:T(8,128)(2,1)S(1)}, bf16[512,256]{1,0:T(8,128)(2,1)S(1)}, u32[]{:S(2)}, u32[]{:S(2)}) collective-permute-start(bf16[512,256]{1,0:T(8,128)(2,1)S(1)} %constant_dynamic-update-slice_fusion), channel_id=1, source_target_pairs={{0,128},{32,160},{64,192},{96,224},{128,256},{160,288},{192,320},{... | collective-permute-start | bytes 786440 | tf_op jit(solution)/shard_map/ppermute | solution.py:19
  18.9 32.1 %collective-permute-start.1 = (bf16[512,256]{1,0:T(8,128)(2,1)S(1)}, bf16[512,256]{1,0:T(8,128)(2,1)S(1)}, u32[]{:S(2)}, u32[]{:S(2)}) collective-permute-start(bf16[512,256]{1,0:T(8,128)(2,1)S(1)} %constant_dynamic-update-slice_fusion), channel_id=1, source_target_pairs={{0,384},{32,416},{64,448},{96,480},{128,0},{160,32},{192,64},{224,... | collective-permute-start | bytes 786440 | tf_op jit(solution)/shard_map/ppermute | solution.py:19
  51.0 29.6 %collective-permute-start.6 = (bf16[3,512,256]{2,1,0:T(8,128)(2,1)S(1)}, bf16[3,512,256]{2,1,0:T(8,128)(2,1)S(1)}, u32[]{:S(2)}, u32[]{:S(2)}) collective-permute-start(bf16[3,512,256]{2,1,0:T(8,128)(2,1)S(1)} %pad_maximum_fusion.refs_0_), channel_id=1, source_target_pairs={{0,96},{32,0},{64,32},{96,64},{128,224},{160,128},{192,160},{224,1... | collective-permute-start | bytes 2359304 | tf_op jit(solution)/shard_map/ppermute | solution.py:19
  53.8 39.1 %collective-permute-start.4 = (bf16[3,512,256]{2,1,0:T(8,128)(2,1)S(1)}, bf16[3,512,256]{2,1,0:T(8,128)(2,1)S(1)}, u32[]{:S(2)}, u32[]{:S(2)}) collective-permute-start(bf16[3,512,256]{2,1,0:T(8,128)(2,1)S(1)} %pad_maximum_fusion.refs_0_), channel_id=1, source_target_pairs={{0,32},{32,64},{64,96},{96,0},{128,160},{160,192},{192,224},{224,1... | collective-permute-start | bytes 2359304 | tf_op jit(solution)/shard_map/ppermute | solution.py:19
  58.1 14.5 %collective-permute-start.2 = (bf16[256,256]{1,0:T(8,128)(2,1)S(1)}, bf16[256,256]{1,0:T(8,128)(2,1)S(1)}, u32[]{:S(2)}, u32[]{:S(2)}) collective-permute-start(bf16[256,256]{1,0:T(8,128)(2,1)S(1)} %slice.220), channel_id=1, source_target_pairs={{0,128},{32,160},{64,192},{96,224},{128,256},{160,288},{192,320},{... | collective-permute-start | bytes 393224 | tf_op jit(solution)/shard_map/ppermute | solution.py:19
  65.6 13.1 %collective-permute-start.3 = (bf16[256,256]{1,0:T(8,128)(2,1)S(1)}, bf16[256,256]{1,0:T(8,128)(2,1)S(1)}, u32[]{:S(2)}, u32[]{:S(2)}) collective-permute-start(bf16[256,256]{1,0:T(8,128)(2,1)S(1)} %slice.221), channel_id=1, source_target_pairs={{0,384},{32,416},{64,448},{96,480},{128,0},{160,32},{192,64},{224,... | collective-permute-start | bytes 393224 | tf_op jit(solution)/shard_map/ppermute | solution.py:19
  90.9 24.0 %collective-permute-start.9 = (bf16[2,512,256]{2,1,0:T(8,128)(2,1)}, bf16[2,512,256]{2,1,0:T(8,128)(2,1)S(1)}, u32[]{:S(2)}, u32[]{:S(2)}) collective-permute-start(bf16[2,512,256]{2,1,0:T(8,128)(2,1)} %pad_maximum_fusion.1), channel_id=1, source_target_pairs={{0,96},{32,0},{64,32},{96,64},{128,224},{160,128},{192,160},{224,1... | collective-permute-start | bytes 1572872 | tf_op jit(solution)/shard_map/ppermute | solution.py:19
  93.7 21.2 %collective-permute-start.8 = (bf16[2,512,256]{2,1,0:T(8,128)(2,1)}, bf16[2,512,256]{2,1,0:T(8,128)(2,1)}, u32[]{:S(2)}, u32[]{:S(2)}) collective-permute-start(bf16[2,512,256]{2,1,0:T(8,128)(2,1)} %slice.222), channel_id=1, source_target_pairs={{0,32},{32,64},{64,96},{96,0},{128,160},{160,192},{192,224},{224,1... | collective-permute-start | bytes 1572872 | tf_op jit(solution)/shard_map/ppermute | solution.py:19
  100.4 35.1 %collective-permute-start.12 = (bf16[2,144,128]{2,1,0:T(8,128)(2,1)}, bf16[2,144,128]{2,1,0:T(8,128)(2,1)}, u32[]{:S(2)}, u32[]{:S(2)}) collective-permute-start(bf16[2,144,128]{2,1,0:T(8,128)(2,1)} %slice.174), channel_id=1, source_target_pairs={{32,0},{64,32},{96,64},{128,96},{160,128},{192,160},{224,192},{256... | collective-permute-start | bytes 221192 | tf_op jit(solution)/shard_map/ppermute | solution.py:24
  102.3 12.6 %collective-permute-start.5 = (bf16[1,512,256]{2,1,0:T(8,128)(2,1)S(1)}, bf16[1,512,256]{2,1,0:T(8,128)(2,1)}, u32[]{:S(2)}, u32[]{:S(2)}) collective-permute-start(bf16[1,512,256]{2,1,0:T(8,128)(2,1)S(1)} %maximum_bitcast_fusion.refs_1_), channel_id=1, source_target_pairs={{0,32},{32,64},{64,96},{96,0},{128,160},{160,192},{192,224},{224,1... | collective-permute-start | bytes 786440 | tf_op jit(solution)/shard_map/ppermute | solution.py:19
  124.4 18.9 %collective-permute-start.10 = (bf16[144,256]{1,0:T(8,128)(2,1)}, bf16[144,256]{1,0:T(8,128)(2,1)S(1)}, u32[]{:S(2)}, u32[]{:S(2)}) collective-permute-start(bf16[144,256]{1,0:T(8,128)(2,1)} %get-tuple-element.27), channel_id=1, source_target_pairs={{0,32},{32,64},{64,96},{96,128},{128,160},{160,192},{192,224},{224... | collective-permute-start | bytes 221192 | tf_op jit(solution)/shard_map/ppermute | solution.py:24
  131.7 11.6 %collective-permute-start.11 = (bf16[16,256]{1,0:T(8,128)(2,1)S(1)}, bf16[16,256]{1,0:T(8,128)(2,1)S(1)}, u32[]{:S(2)}, u32[]{:S(2)}) collective-permute-start(bf16[16,256]{1,0:T(8,128)(2,1)S(1)} %get-tuple-element.28), channel_id=1, source_target_pairs={{32,0},{64,32},{96,64},{128,96},{160,128},{192,160},{224,192},{256... | collective-permute-start | bytes 24584 | tf_op jit(solution)/shard_map/ppermute | solution.py:24
  159.5 21.3 %collective-permute-start.16 = (bf16[288,512]{1,0:T(8,128)(2,1)S(1)}, bf16[288,512]{1,0:T(8,128)(2,1)S(1)}, u32[]{:S(2)}, u32[]{:S(2)}) collective-permute-start(bf16[288,512]{1,0:T(8,128)(2,1)S(1)} %get-tuple-element.42), channel_id=1, source_target_pairs={{0,96},{32,0},{64,32},{96,64},{128,224},{160,128},{192,160},{224,1... | collective-permute-start | bytes 884744 | tf_op jit(solution)/shard_map/ppermute | solution.py:19
  166.7 14.1 %collective-permute-start.18 = (bf16[160,512]{1,0:T(8,128)(2,1)S(1)}, bf16[160,512]{1,0:T(8,128)(2,1)S(1)}, u32[]{:S(2)}, u32[]{:S(2)}) collective-permute-start(bf16[160,512]{1,0:T(8,128)(2,1)S(1)} %pad_maximum_fusion.4), channel_id=1, source_target_pairs={{0,32},{32,64},{64,96},{96,0},{128,160},{160,192},{192,224},{224,1... | collective-permute-start | bytes 491528 | tf_op jit(solution)/shard_map/ppermute | solution.py:19
  174.9 17.6 %collective-permute-start.14 = (bf16[768,512]{1,0:T(8,128)(2,1)S(1)}, bf16[768,512]{1,0:T(8,128)(2,1)S(1)}, u32[]{:S(2)}, u32[]{:S(2)}) collective-permute-start(bf16[768,512]{1,0:T(8,128)(2,1)S(1)} %get-tuple-element.39), channel_id=1, source_target_pairs={{0,32},{32,64},{64,96},{96,0},{128,160},{160,192},{192,224},{224,1... | collective-permute-start | bytes 2359304 | tf_op jit(solution)/shard_map/ppermute | solution.py:19
  176.8 20.0 %collective-permute-start.13 = (bf16[768,512]{1,0:T(8,128)(2,1)S(1)}, bf16[768,512]{1,0:T(8,128)(2,1)S(1)}, u32[]{:S(2)}, u32[]{:S(2)}) collective-permute-start(bf16[768,512]{1,0:T(8,128)(2,1)S(1)} %get-tuple-element.37), channel_id=1, source_target_pairs={{0,96},{32,0},{64,32},{96,64},{128,224},{160,128},{192,160},{224,1... | collective-permute-start | bytes 2359304 | tf_op jit(solution)/shard_map/ppermute | solution.py:19
  180.9 20.0 %collective-permute-start.22 = (bf16[128,512]{1,0:T(8,128)(2,1)S(1)}, bf16[128,512]{1,0:T(8,128)(2,1)S(1)}, u32[]{:S(2)}, u32[]{:S(2)}) collective-permute-start(bf16[128,512]{1,0:T(8,128)(2,1)S(1)} %get-tuple-element.64), channel_id=1, source_target_pairs={{0,96},{32,0},{64,32},{96,64},{128,224},{160,128},{192,160},{224,1... | collective-permute-start | bytes 393224 | tf_op jit(solution)/shard_map/ppermute | solution.py:19
  192.6 31.2 %collective-permute-start.15 = (bf16[384,512]{1,0:T(8,128)(2,1)S(1)}, bf16[384,512]{1,0:T(8,128)(2,1)S(1)}, u32[]{:S(2)}, u32[]{:S(2)}) collective-permute-start(bf16[384,512]{1,0:T(8,128)(2,1)S(1)} %add_convert_fusion.1), channel_id=1, source_target_pairs={{0,32},{32,64},{64,96},{96,0},{128,160},{160,192},{192,224},{224,1... | collective-permute-start | bytes 1179656 | tf_op jit(solution)/shard_map/ppermute | solution.py:19
  197.0 26.9 %collective-permute-start.20 = (bf16[384,512]{1,0:T(8,128)(2,1)S(1)}, bf16[384,512]{1,0:T(8,128)(2,1)S(1)}, u32[]{:S(2)}, u32[]{:S(2)}) collective-permute-start(bf16[384,512]{1,0:T(8,128)(2,1)S(1)} %add_convert_fusion), channel_id=1, source_target_pairs={{0,96},{32,0},{64,32},{96,64},{128,224},{160,128},{192,160},{224,1... | collective-permute-start | bytes 1179656 | tf_op jit(solution)/shard_map/ppermute | solution.py:19
  201.0 22.9 %collective-permute-start.19 = (bf16[160,512]{1,0:T(8,128)(2,1)S(1)}, bf16[160,512]{1,0:T(8,128)(2,1)S(1)}, u32[]{:S(2)}, u32[]{:S(2)}) collective-permute-start(bf16[160,512]{1,0:T(8,128)(2,1)S(1)} %get-tuple-element.65), channel_id=1, source_target_pairs={{0,128},{32,160},{64,192},{96,224},{128,256},{160,288},{192,320},{... | collective-permute-start | bytes 491528 | tf_op jit(solution)/shard_map/ppermute | solution.py:19
  204.9 35.3 %collective-permute-start.23 = (bf16[160,512]{1,0:T(8,128)(2,1)S(1)}, bf16[160,512]{1,0:T(8,128)(2,1)S(1)}, u32[]{:S(2)}, u32[]{:S(2)}) collective-permute-start(bf16[160,512]{1,0:T(8,128)(2,1)S(1)} %get-tuple-element.66), channel_id=1, source_target_pairs={{0,384},{32,416},{64,448},{96,480},{128,0},{160,32},{192,64},{224,... | collective-permute-start | bytes 491528 | tf_op jit(solution)/shard_map/ppermute | solution.py:19
  224.3 22.2 %collective-permute-start.21 = (bf16[288,512]{1,0:T(8,128)(2,1)S(1)}, bf16[288,512]{1,0:T(8,128)(2,1)S(1)}, u32[]{:S(2)}, u32[]{:S(2)}) collective-permute-start(bf16[288,512]{1,0:T(8,128)(2,1)S(1)} %pad_maximum_fusion.2), channel_id=1, source_target_pairs={{0,128},{32,160},{64,192},{96,224},{128,256},{160,288},{192,320},{... | collective-permute-start | bytes 884744 | tf_op jit(solution)/shard_map/ppermute | solution.py:19
  240.3 14.5 %collective-permute-start.24 = (bf16[256,512]{1,0:T(8,128)(2,1)S(1)}, bf16[256,512]{1,0:T(8,128)(2,1)S(1)}, u32[]{:S(2)}, u32[]{:S(2)}) collective-permute-start(bf16[256,512]{1,0:T(8,128)(2,1)S(1)} %pad_maximum_fusion.3), channel_id=1, source_target_pairs={{0,384},{32,416},{64,448},{96,480},{128,0},{160,32},{192,64},{224,... | collective-permute-start | bytes 786440 | tf_op jit(solution)/shard_map/ppermute | solution.py:19
  (10 other events, 166.0 us)
Sparse Core Ops, SparseCore 0:
  10.1 101.1 all-gather.1

commit v2 on v1

--- a/solution.py
+++ b/solution.py
@@ -10,6 +10,10 @@
 
 BF = jnp.bfloat16
 F32 = jnp.float32
+
+
+def in_hbm(value):
+    return pltpu.with_memory_space_constraint(value, pltpu.HBM)
 
 
 def dp_move(value, dzh, dx):
@@ -228,17 +232,19 @@
 
 
 def reduce_grads(idx, features, outgoing, small):
-    far = backward_matmul(GROUPS[0], idx, features, outgoing, small)
+    far = backward_matmul(GROUPS[0], idx, features, outgoing, in_hbm(small))
     from_west, from_east = far_first = ring_first(far)
     near = backward_matmul(GROUPS[1], idx, features, outgoing)
     near_first = ring_first(near)
     east2, west2 = ring_second(far, far_first)
+    from_west, from_east = lax.optimization_barrier((from_west, from_east))
     low = add(far[4][:HALF], from_east[HALF : 2 * HALF], east2[:HALF]).astype(BF)
     high = add(far[4][HALF:], from_west[HALF : 2 * HALF], west2).astype(BF)
     small = ring_sum(small, from_west[2 * HALF :], from_east[2 * HALF :], east2[HALF:])
-    row = small_rows(small)
-    from_south = dp_move(jnp.concatenate([low, row]), 1, 0)
-    from_north = dp_move(jnp.concatenate([high, row]), -1, 0)
+    low = jnp.concatenate([low, small_rows(small)])
+    high = jnp.concatenate([high, small_rows(small)])
+    from_south = dp_move(low, 1, 0)
+    from_north = dp_move(high, -1, 0)
     east2, west2 = ring_second(near, near_first)
     from_west, from_east = near_first
     low = add(near[4][: 3 * HALF], from_east[3 * HALF :], east2)
@@ -419,17 +425,17 @@
     meta = jnp.concatenate([(dp * count).reshape(1).astype(jnp.int32), lengths])
 
     features = lax.all_gather(inputs.reshape(seqs * count, local_width), "shard", axis=0)
-    features = pltpu.with_memory_space_constraint(features, pltpu.HBM)
+    features = in_hbm(features)
     panels = gather_panels(jnp.concatenate([key_panel, value_panel], axis=1))
     after = shifted(cotangent[:, :144], -1)
     up, product_grad, bands = cotangent_terms(meta, cotangent, after, medium_filters)
 
     taps = jnp.pad(short_filters.reshape(256, 7), ((0, 0), (0, 1)))
     kv, prev, head = forward_matmul(idx, features, taps, panels)
-    prev = shifted(prev, 1)
-    head = shifted(head, -1)
-    outgoing, product, sums = middle_terms(kv, prev, head, product_grad, taps)
-
+    prev = in_hbm(shifted(prev, 1))
+    head = in_hbm(shifted(head, -1))
+    outgoing, product, sums = middle_terms(in_hbm(kv), prev, head, product_grad, taps)
+    outgoing = in_hbm(outgoing)
     mixed, small = response_terms(meta, product, up, bands, sums)
     key_grad, value_grad, small = reduce_grads(idx, features, outgoing, small)
     short_grad = small[:16].reshape(2, 8, channels)[:, :7].transpose(0, 2, 1)

time: 265 us -> 260 us (0.981)
  the two profiles are of different devices: /device:TPU:22 before, /device:TPU:8 now
where the time goes in v2:
time: 260 us; the launch traced here: 259 us
  starting transfers between devices  109 us (42%)
  waiting for transfers between devices  88.4 us (34%)
  Pallas kernels  29.4 us (11%)
  between operations  14.6 us (6%)
  local copies, waits for them, and re-layouts  11.8 us (5%)
  other arithmetic  5.24 us (2%)
    ppermute x22, starting transfers between devices, dp_move(): return lax.ppermute(value, 'dp', pairs)  106 us
    ppermute x22, waiting for transfers between devices, dp_move(): return lax.ppermute(value, 'dp', pairs)  87.7 us
    pallas_call x2, Pallas kernels, backward_matmul(): pl.pallas_call(functools.partial(backward_kernel, rels), out_shape=[sent,...  9.06 us
    pallas_call x1, Pallas kernels, forward_matmul(): pl.pallas_call(forward_kernel, out_shape=[jax.ShapeDtypeStruct((width, ro...  8.86 us
    pallas_call x1, Pallas kernels, middle_terms(): pl.pallas_call(middle_kernel, out_shape=[jax.ShapeDtypeStruct((256, 512),...  6.23 us
    unnamed x17, local copies, waits for them, and re-layouts  5.87 us
  transfers between devices with their start and end apart: 26, of which 12 were waited for; matrix products, arithmetic and copies ran while one was open for 5% of the time, Pallas kernels for 7%

profile of v2, /device:TPU:8, one launch (start us, length us, event | category | flops | bytes accessed | tf_op | source)
XLA Modules:
  0.0 259.0 jit_solution(2927970696586139054)
XLA Ops:
  9.8 9.1 %collective-permute-start = (bf16[512,256]{1,0:T(8,128)(2,1)S(1)}, bf16[512,256]{1,0:T(8,128)(2,1)S(1)}, u32[]{:S(2)}, u32[]{:S(2)}) collective-permute-start(bf16[512,256]{1,0:T(8,128)(2,1)S(1)} %constant_dynamic-update-slice_fusion), channel_id=1, source_target_pairs={{0,128},{32,160},{64,192},{96,224},{128,256},{160,288},{192,320},{... | collective-permute-start | bytes 786440 | tf_op jit(solution)/shard_map/ppermute | solution.py:23
  18.9 5.6 %collective-permute-start.1 = (bf16[512,256]{1,0:T(8,128)(2,1)S(1)}, bf16[512,256]{1,0:T(8,128)(2,1)S(1)}, u32[]{:S(2)}, u32[]{:S(2)}) collective-permute-start(bf16[512,256]{1,0:T(8,128)(2,1)S(1)} %constant_dynamic-update-slice_fusion), channel_id=1, source_target_pairs={{0,384},{32,416},{64,448},{96,480},{128,0},{160,32},{192,64},{224,... | collective-permute-start | bytes 786440 | tf_op jit(solution)/shard_map/ppermute | solution.py:23
  24.4 7.6 %collective-permute-done = bf16[512,256]{1,0:T(8,128)(2,1)S(1)} collective-permute-done((bf16[512,256]{1,0:T(8,128)(2,1)S(1)}, bf16[512,256]{1,0:T(8,128)(2,1)S(1)}, u32[]{:S(2)}, u32[]{:S(2)}) %collective-permute-start) | collective-permute-done | bytes 262176 | tf_op jit(solution)/shard_map/ppermute | solution.py:23
  32.1 17.7 %collective-permute-done.1 = bf16[512,256]{1,0:T(8,128)(2,1)S(1)} collective-permute-done((bf16[512,256]{1,0:T(8,128)(2,1)S(1)}, bf16[512,256]{1,0:T(8,128)(2,1)S(1)}, u32[]{:S(2)}, u32[]{:S(2)}) %collective-permute-start.1) | collective-permute-done | bytes 262176 | tf_op jit(solution)/shard_map/ppermute | solution.py:23
  49.8 4.7 %collective-permute-start.6 = (bf16[3,512,256]{2,1,0:T(8,128)(2,1)S(1)}, bf16[3,512,256]{2,1,0:T(8,128)(2,1)S(1)}, u32[]{:S(2)}, u32[]{:S(2)}) collective-permute-start(bf16[3,512,256]{2,1,0:T(8,128)(2,1)S(1)} %pad_maximum_fusion.refs_0_), channel_id=1, source_target_pairs={{0,96},{32,0},{64,32},{96,64},{128,224},{160,128},{192,160},{224,1... | collective-permute-start | bytes 2359304 | tf_op jit(solution)/shard_map/ppermute | solution.py:23
  56.5 6.2 %collective-permute-start.2 = (bf16[256,256]{1,0:T(8,128)(2,1)S(1)}, bf16[256,256]{1,0:T(8,128)(2,1)S(1)}, u32[]{:S(2)}, u32[]{:S(2)}) collective-permute-start(bf16[256,256]{1,0:T(8,128)(2,1)S(1)} %slice.220), channel_id=1, source_target_pairs={{0,128},{32,160},{64,192},{96,224},{128,256},{160,288},{192,320},{... | collective-permute-start | bytes 393224 | tf_op jit(solution)/shard_map/ppermute | solution.py:23
  68.5 6.8 %collective-permute-done.3 = bf16[256,256]{1,0:T(8,128)(2,1)S(1)} collective-permute-done((bf16[256,256]{1,0:T(8,128)(2,1)S(1)}, bf16[256,256]{1,0:T(8,128)(2,1)S(1)}, u32[]{:S(2)}, u32[]{:S(2)}) %collective-permute-start.3) | collective-permute-done | bytes 131104 | tf_op jit(solution)/shard_map/ppermute | solution.py:23
  75.3 4.9 %collective-permute-start.7 = (bf16[1,512,256]{2,1,0:T(8,128)(2,1)S(1)}, bf16[1,512,256]{2,1,0:T(8,128)(2,1)S(1)}, u32[]{:S(2)}, u32[]{:S(2)}) collective-permute-start(bf16[1,512,256]{2,1,0:T(8,128)(2,1)S(1)} %maximum_bitcast_fusion.refs_1_), channel_id=1, source_target_pairs={{0,96},{32,0},{64,32},{96,64},{128,224},{160,128},{192,160},{224,1... | collective-permute-start | bytes 786440 | tf_op jit(solution)/shard_map/ppermute | solution.py:23
  80.2 5.6 %collective-permute-done.7.refs_5_ = bf16[1,512,256]{2,1,0:T(8,128)(2,1)S(1)} collective-permute-done((bf16[1,512,256]{2,1,0:T(8,128)(2,1)S(1)}, bf16[1,512,256]{2,1,0:T(8,128)(2,1)S(1)}, u32[]{:S(2)}, u32[]{:S(2)}) %collective-permute-start.7) | collective-permute-done | bytes 262176 | tf_op jit(solution)/shard_map/ppermute | solution.py:23
  86.7 5.6 %collective-permute-start.9 = (bf16[2,512,256]{2,1,0:T(8,128)(2,1)}, bf16[2,512,256]{2,1,0:T(8,128)(2,1)S(1)}, u32[]{:S(2)}, u32[]{:S(2)}) collective-permute-start(bf16[2,512,256]{2,1,0:T(8,128)(2,1)} %pad_maximum_fusion.1), channel_id=1, source_target_pairs={{0,96},{32,0},{64,32},{96,64},{128,224},{160,128},{192,160},{224,1... | collective-permute-start | bytes 1572872 | tf_op jit(solution)/shard_map/ppermute | solution.py:23
  107.2 7.6 %collective-permute-done.5.refs_3_ = bf16[1,512,256]{2,1,0:T(8,128)(2,1)} collective-permute-done((bf16[1,512,256]{2,1,0:T(8,128)(2,1)S(1)}, bf16[1,512,256]{2,1,0:T(8,128)(2,1)}, u32[]{:S(2)}, u32[]{:S(2)}) %collective-permute-start.5) | collective-permute-done | bytes 262176 | tf_op jit(solution)/shard_map/ppermute | solution.py:23
  114.8 8.9 %shard_map.110 = (bf16[256,512]{1,0:T(8,128)(2,1)S(1)}, bf16[144,256]{1,0:T(8,128)(2,1)}, bf16[16,256]{1,0:T(8,128)(2,1)S(1)}) custom-call(s32[2]{0:T(128)S(1)} %pad_add_fusion.1.idx_ref, bf16[32,512,256]{2,1,0:T(8,128)(2,1)} %all-gather.2.cloned.1.call-done.x_ref, f32[256,8]{1,0:T(8,128)S(1)} %pad.5.taps_ref, ...), custom_call_target="tpu_custom_call" | custom-call | tf_op jit(solution)/shard_map/pallas_call | solution.py:102
  131.9 6.2 %shard_map.112 = (bf16[256,512]{1,0:T(8,128)(2,1)}, bf16[128,768]{1,0:T(8,128)(2,1)}, f32[16,128]{1,0:T(8,128)}) custom-call(bf16[256,512]{1,0:T(8,128)(2,1)} %copy-done.1, bf16[144,256]{1,0:T(8,128)(2,1)} %copy-done.2, bf16[16,256]{1,0:T(8,128)(2,1)} %copy-done.5, f32[128,768]{1,0:T(8,128)} %get-tuple-element.31.grad_ref, f32[256,8]{1,0:T(8,128)} %copy-done), custom_call_target="tpu_custom_call" | custom-call | tf_op jit(solution)/shard_map/pallas_call | solution.py:363
  148.8 12.5 %collective-permute-start.17 = (bf16[288,512]{1,0:T(8,128)(2,1)S(1)}, bf16[288,512]{1,0:T(8,128)(2,1)S(1)}, u32[]{:S(2)}, u32[]{:S(2)}) collective-permute-start(bf16[288,512]{1,0:T(8,128)(2,1)S(1)} %get-tuple-element.45), channel_id=1, source_target_pairs={{0,96},{32,0},{64,32},{96,64},{128,224},{160,128},{192,160},{224,1... | collective-permute-start | bytes 884744 | tf_op jit(solution)/shard_map/ppermute | solution.py:23
  161.3 5.8 %shard_map.114 = (bf16[768,512]{1,0:T(8,128)(2,1)S(1)}, bf16[768,512]{1,0:T(8,128)(2,1)S(1)}, bf16[384,512]{1,0:T(8,128)(2,1)S(1)}, bf16[384,512]{1,0:T(8,128)(2,1)S(1)}, bf16[768,512]{1,0:T(8,128)(2,1)S(1)}) custom-call(s32[2]{0:T(128)S(1)} %pad_add_fusion.1.idx_ref, bf16[32,512,256]{2,1,0:T(8,128)(2,1)} %all-gather.2.cloned.1.call-done.x_ref, ...), custom_call_target="tpu_custom_call" | custom-call | tf_op jit(solution)/shard_map/pallas_call | solution.py:195
  169.1 5.1 %collective-permute-start.13 = (bf16[768,512]{1,0:T(8,128)(2,1)S(1)}, bf16[768,512]{1,0:T(8,128)(2,1)S(1)}, u32[]{:S(2)}, u32[]{:S(2)}) collective-permute-start(bf16[768,512]{1,0:T(8,128)(2,1)S(1)} %get-tuple-element.39), channel_id=1, source_target_pairs={{0,96},{32,0},{64,32},{96,64},{128,224},{160,128},{192,160},{224,1... | collective-permute-start | bytes 2359304 | tf_op jit(solution)/shard_map/ppermute | solution.py:23
  176.3 5.1 %collective-permute-start.22 = (bf16[128,512]{1,0:T(8,128)(2,1)S(1)}, bf16[128,512]{1,0:T(8,128)(2,1)S(1)}, u32[]{:S(2)}, u32[]{:S(2)}) collective-permute-start(bf16[128,512]{1,0:T(8,128)(2,1)S(1)} %add_convert_fusion.3), channel_id=1, source_target_pairs={{0,96},{32,0},{64,32},{96,64},{128,224},{160,128},{192,160},{224,1... | collective-permute-start | bytes 393224 | tf_op jit(solution)/shard_map/ppermute | solution.py:23
  181.4 8.4 %collective-permute-done.18 = bf16[160,512]{1,0:T(8,128)(2,1)S(1)} collective-permute-done((bf16[160,512]{1,0:T(8,128)(2,1)S(1)}, bf16[160,512]{1,0:T(8,128)(2,1)S(1)}, u32[]{:S(2)}, u32[]{:S(2)}) %collective-permute-start.18) | collective-permute-done | bytes 163872 | tf_op jit(solution)/shard_map/ppermute | solution.py:23
  193.3 4.9 %collective-permute-start.20 = (bf16[384,512]{1,0:T(8,128)(2,1)S(1)}, bf16[384,512]{1,0:T(8,128)(2,1)S(1)}, u32[]{:S(2)}, u32[]{:S(2)}) collective-permute-start(bf16[384,512]{1,0:T(8,128)(2,1)S(1)} %add_convert_fusion), channel_id=1, source_target_pairs={{0,96},{32,0},{64,32},{96,64},{128,224},{160,128},{192,160},{224,1... | collective-permute-start | bytes 1179656 | tf_op jit(solution)/shard_map/ppermute | solution.py:23
  198.3 7.9 %collective-permute-start.19 = (bf16[160,512]{1,0:T(8,128)(2,1)S(1)}, bf16[160,512]{1,0:T(8,128)(2,1)S(1)}, u32[]{:S(2)}, u32[]{:S(2)}) collective-permute-start(bf16[160,512]{1,0:T(8,128)(2,1)S(1)} %get-tuple-element.69), channel_id=1, source_target_pairs={{0,128},{32,160},{64,192},{96,224},{128,256},{160,288},{192,320},{... | collective-permute-start | bytes 491528 | tf_op jit(solution)/shard_map/ppermute | solution.py:23
  208.1 6.3 %collective-permute-done.19 = bf16[160,512]{1,0:T(8,128)(2,1)S(1)} collective-permute-done((bf16[160,512]{1,0:T(8,128)(2,1)S(1)}, bf16[160,512]{1,0:T(8,128)(2,1)S(1)}, u32[]{:S(2)}, u32[]{:S(2)}) %collective-permute-start.19) | collective-permute-done | bytes 163872 | tf_op jit(solution)/shard_map/ppermute | solution.py:23
  214.8 7.1 %collective-permute-start.21 = (bf16[288,512]{1,0:T(8,128)(2,1)S(1)}, bf16[288,512]{1,0:T(8,128)(2,1)S(1)}, u32[]{:S(2)}, u32[]{:S(2)}) collective-permute-start(bf16[288,512]{1,0:T(8,128)(2,1)S(1)} %pad_maximum_fusion.2), channel_id=1, source_target_pairs={{0,128},{32,160},{64,192},{96,224},{128,256},{160,288},{192,320},{... | collective-permute-start | bytes 884744 | tf_op jit(solution)/shard_map/ppermute | solution.py:23
  225.8 11.5 %collective-permute-done.21 = bf16[288,512]{1,0:T(8,128)(2,1)S(1)} collective-permute-done((bf16[288,512]{1,0:T(8,128)(2,1)S(1)}, bf16[288,512]{1,0:T(8,128)(2,1)S(1)}, u32[]{:S(2)}, u32[]{:S(2)}) %collective-permute-start.21) | collective-permute-done | bytes 294944 | tf_op jit(solution)/shard_map/ppermute | solution.py:23
  238.0 11.8 %collective-permute-done.24 = bf16[256,512]{1,0:T(8,128)(2,1)S(1)} collective-permute-done((bf16[256,512]{1,0:T(8,128)(2,1)S(1)}, bf16[256,512]{1,0:T(8,128)(2,1)S(1)}, u32[]{:S(2)}, u32[]{:S(2)}) %collective-permute-start.24) | collective-permute-done | bytes 262176 | tf_op jit(solution)/shard_map/ppermute | solution.py:23
  (96 shorter events, 61.7 us)
Async XLA Ops:
  7.2 107.6 %all-gather.2.cloned.1.call-start = ((), (), s32[]{:S(2)}) async-start(), calls=%async_computation | async-start | bytes 8650752 | tf_op jit(solution)/shard_map/all_gather | solution.py:427
  9.8 22.3 %collective-permute-start = (bf16[512,256]{1,0:T(8,128)(2,1)S(1)}, bf16[512,256]{1,0:T(8,128)(2,1)S(1)}, u32[]{:S(2)}, u32[]{:S(2)}) collective-permute-start(bf16[512,256]{1,0:T(8,128)(2,1)S(1)} %constant_dynamic-update-slice_fusion), channel_id=1, source_target_pairs={{0,128},{32,160},{64,192},{96,224},{128,256},{160,288},{192,320},{... | collective-permute-start | bytes 786440 | tf_op jit(solution)/shard_map/ppermute | solution.py:23
  18.9 30.9 %collective-permute-start.1 = (bf16[512,256]{1,0:T(8,128)(2,1)S(1)}, bf16[512,256]{1,0:T(8,128)(2,1)S(1)}, u32[]{:S(2)}, u32[]{:S(2)}) collective-permute-start(bf16[512,256]{1,0:T(8,128)(2,1)S(1)} %constant_dynamic-update-slice_fusion), channel_id=1, source_target_pairs={{0,384},{32,416},{64,448},{96,480},{128,0},{160,32},{192,64},{224,... | collective-permute-start | bytes 786440 | tf_op jit(solution)/shard_map/ppermute | solution.py:23
  49.8 30.4 %collective-permute-start.6 = (bf16[3,512,256]{2,1,0:T(8,128)(2,1)S(1)}, bf16[3,512,256]{2,1,0:T(8,128)(2,1)S(1)}, u32[]{:S(2)}, u32[]{:S(2)}) collective-permute-start(bf16[3,512,256]{2,1,0:T(8,128)(2,1)S(1)} %pad_maximum_fusion.refs_0_), channel_id=1, source_target_pairs={{0,96},{32,0},{64,32},{96,64},{128,224},{160,128},{192,160},{224,1... | collective-permute-start | bytes 2359304 | tf_op jit(solution)/shard_map/ppermute | solution.py:23
  54.5 37.8 %collective-permute-start.4 = (bf16[3,512,256]{2,1,0:T(8,128)(2,1)S(1)}, bf16[3,512,256]{2,1,0:T(8,128)(2,1)S(1)}, u32[]{:S(2)}, u32[]{:S(2)}) collective-permute-start(bf16[3,512,256]{2,1,0:T(8,128)(2,1)S(1)} %pad_maximum_fusion.refs_0_), channel_id=1, source_target_pairs={{0,32},{32,64},{64,96},{96,0},{128,160},{160,192},{192,224},{224,1... | collective-permute-start | bytes 2359304 | tf_op jit(solution)/shard_map/ppermute | solution.py:23
  56.5 12.1 %collective-permute-start.2 = (bf16[256,256]{1,0:T(8,128)(2,1)S(1)}, bf16[256,256]{1,0:T(8,128)(2,1)S(1)}, u32[]{:S(2)}, u32[]{:S(2)}) collective-permute-start(bf16[256,256]{1,0:T(8,128)(2,1)S(1)} %slice.220), channel_id=1, source_target_pairs={{0,128},{32,160},{64,192},{96,224},{128,256},{160,288},{192,320},{... | collective-permute-start | bytes 393224 | tf_op jit(solution)/shard_map/ppermute | solution.py:23
  62.6 12.7 %collective-permute-start.3 = (bf16[256,256]{1,0:T(8,128)(2,1)S(1)}, bf16[256,256]{1,0:T(8,128)(2,1)S(1)}, u32[]{:S(2)}, u32[]{:S(2)}) collective-permute-start(bf16[256,256]{1,0:T(8,128)(2,1)S(1)} %slice.221), channel_id=1, source_target_pairs={{0,384},{32,416},{64,448},{96,480},{128,0},{160,32},{192,64},{224,... | collective-permute-start | bytes 393224 | tf_op jit(solution)/shard_map/ppermute | solution.py:23
  75.3 10.5 %collective-permute-start.7 = (bf16[1,512,256]{2,1,0:T(8,128)(2,1)S(1)}, bf16[1,512,256]{2,1,0:T(8,128)(2,1)S(1)}, u32[]{:S(2)}, u32[]{:S(2)}) collective-permute-start(bf16[1,512,256]{2,1,0:T(8,128)(2,1)S(1)} %maximum_bitcast_fusion.refs_1_), channel_id=1, source_target_pairs={{0,96},{32,0},{64,32},{96,64},{128,224},{160,128},{192,160},{224,1... | collective-permute-start | bytes 786440 | tf_op jit(solution)/shard_map/ppermute | solution.py:23
  86.7 28.1 %collective-permute-start.9 = (bf16[2,512,256]{2,1,0:T(8,128)(2,1)}, bf16[2,512,256]{2,1,0:T(8,128)(2,1)S(1)}, u32[]{:S(2)}, u32[]{:S(2)}) collective-permute-start(bf16[2,512,256]{2,1,0:T(8,128)(2,1)} %pad_maximum_fusion.1), channel_id=1, source_target_pairs={{0,96},{32,0},{64,32},{96,64},{128,224},{160,128},{192,160},{224,1... | collective-permute-start | bytes 1572872 | tf_op jit(solution)/shard_map/ppermute | solution.py:23
  93.2 21.6 %collective-permute-start.8 = (bf16[2,512,256]{2,1,0:T(8,128)(2,1)}, bf16[2,512,256]{2,1,0:T(8,128)(2,1)}, u32[]{:S(2)}, u32[]{:S(2)}) collective-permute-start(bf16[2,512,256]{2,1,0:T(8,128)(2,1)} %slice.222), channel_id=1, source_target_pairs={{0,32},{32,64},{64,96},{96,0},{128,160},{160,192},{192,224},{224,1... | collective-permute-start | bytes 1572872 | tf_op jit(solution)/shard_map/ppermute | solution.py:23
  96.6 32.2 %collective-permute-start.12 = (bf16[2,144,128]{2,1,0:T(8,128)(2,1)}, bf16[2,144,128]{2,1,0:T(8,128)(2,1)}, u32[]{:S(2)}, u32[]{:S(2)}) collective-permute-start(bf16[2,144,128]{2,1,0:T(8,128)(2,1)} %slice.174), channel_id=1, source_target_pairs={{32,0},{64,32},{96,64},{128,96},{160,128},{192,160},{224,192},{256... | collective-permute-start | bytes 221192 | tf_op jit(solution)/shard_map/ppermute | solution.py:28
  97.9 16.9 %collective-permute-start.5 = (bf16[1,512,256]{2,1,0:T(8,128)(2,1)S(1)}, bf16[1,512,256]{2,1,0:T(8,128)(2,1)}, u32[]{:S(2)}, u32[]{:S(2)}) collective-permute-start(bf16[1,512,256]{2,1,0:T(8,128)(2,1)S(1)} %maximum_bitcast_fusion.refs_1_), channel_id=1, source_target_pairs={{0,32},{32,64},{64,96},{96,0},{128,160},{160,192},{192,224},{224,1... | collective-permute-start | bytes 786440 | tf_op jit(solution)/shard_map/ppermute | solution.py:23
  144.3 29.9 %collective-permute-start.16 = (bf16[288,512]{1,0:T(8,128)(2,1)S(1)}, bf16[288,512]{1,0:T(8,128)(2,1)S(1)}, u32[]{:S(2)}, u32[]{:S(2)}) collective-permute-start(bf16[288,512]{1,0:T(8,128)(2,1)S(1)} %get-tuple-element.44), channel_id=1, source_target_pairs={{0,32},{32,64},{64,96},{96,0},{128,160},{160,192},{192,224},{224,1... | collective-permute-start | bytes 884744 | tf_op jit(solution)/shard_map/ppermute | solution.py:23
  148.8 27.4 %collective-permute-start.17 = (bf16[288,512]{1,0:T(8,128)(2,1)S(1)}, bf16[288,512]{1,0:T(8,128)(2,1)S(1)}, u32[]{:S(2)}, u32[]{:S(2)}) collective-permute-start(bf16[288,512]{1,0:T(8,128)(2,1)S(1)} %get-tuple-element.45), channel_id=1, source_target_pairs={{0,96},{32,0},{64,32},{96,64},{128,224},{160,128},{192,160},{224,1... | collective-permute-start | bytes 884744 | tf_op jit(solution)/shard_map/ppermute | solution.py:23
  167.1 23.3 %collective-permute-start.14 = (bf16[768,512]{1,0:T(8,128)(2,1)S(1)}, bf16[768,512]{1,0:T(8,128)(2,1)S(1)}, u32[]{:S(2)}, u32[]{:S(2)}) collective-permute-start(bf16[768,512]{1,0:T(8,128)(2,1)S(1)} %get-tuple-element.41), channel_id=1, source_target_pairs={{0,32},{32,64},{64,96},{96,0},{128,160},{160,192},{192,224},{224,1... | collective-permute-start | bytes 2359304 | tf_op jit(solution)/shard_map/ppermute | solution.py:23
  169.1 24.1 %collective-permute-start.13 = (bf16[768,512]{1,0:T(8,128)(2,1)S(1)}, bf16[768,512]{1,0:T(8,128)(2,1)S(1)}, u32[]{:S(2)}, u32[]{:S(2)}) collective-permute-start(bf16[768,512]{1,0:T(8,128)(2,1)S(1)} %get-tuple-element.39), channel_id=1, source_target_pairs={{0,96},{32,0},{64,32},{96,64},{128,224},{160,128},{192,160},{224,1... | collective-permute-start | bytes 2359304 | tf_op jit(solution)/shard_map/ppermute | solution.py:23
  174.3 15.6 %collective-permute-start.18 = (bf16[160,512]{1,0:T(8,128)(2,1)S(1)}, bf16[160,512]{1,0:T(8,128)(2,1)S(1)}, u32[]{:S(2)}, u32[]{:S(2)}) collective-permute-start(bf16[160,512]{1,0:T(8,128)(2,1)S(1)} %pad_maximum_fusion.4), channel_id=1, source_target_pairs={{0,32},{32,64},{64,96},{96,0},{128,160},{160,192},{192,224},{224,1... | collective-permute-start | bytes 491528 | tf_op jit(solution)/shard_map/ppermute | solution.py:23
  176.3 14.1 %collective-permute-start.22 = (bf16[128,512]{1,0:T(8,128)(2,1)S(1)}, bf16[128,512]{1,0:T(8,128)(2,1)S(1)}, u32[]{:S(2)}, u32[]{:S(2)}) collective-permute-start(bf16[128,512]{1,0:T(8,128)(2,1)S(1)} %add_convert_fusion.3), channel_id=1, source_target_pairs={{0,96},{32,0},{64,32},{96,64},{128,224},{160,128},{192,160},{224,1... | collective-permute-start | bytes 393224 | tf_op jit(solution)/shard_map/ppermute | solution.py:23
  190.6 23.8 %collective-permute-start.15 = (bf16[384,512]{1,0:T(8,128)(2,1)S(1)}, bf16[384,512]{1,0:T(8,128)(2,1)S(1)}, u32[]{:S(2)}, u32[]{:S(2)}) collective-permute-start(bf16[384,512]{1,0:T(8,128)(2,1)S(1)} %add_convert_fusion.1), channel_id=1, source_target_pairs={{0,32},{32,64},{64,96},{96,0},{128,160},{160,192},{192,224},{224,1... | collective-permute-start | bytes 1179656 | tf_op jit(solution)/shard_map/ppermute | solution.py:23
  193.3 21.1 %collective-permute-start.20 = (bf16[384,512]{1,0:T(8,128)(2,1)S(1)}, bf16[384,512]{1,0:T(8,128)(2,1)S(1)}, u32[]{:S(2)}, u32[]{:S(2)}) collective-permute-start(bf16[384,512]{1,0:T(8,128)(2,1)S(1)} %add_convert_fusion), channel_id=1, source_target_pairs={{0,96},{32,0},{64,32},{96,64},{128,224},{160,128},{192,160},{224,1... | collective-permute-start | bytes 1179656 | tf_op jit(solution)/shard_map/ppermute | solution.py:23
  198.3 16.1 %collective-permute-start.19 = (bf16[160,512]{1,0:T(8,128)(2,1)S(1)}, bf16[160,512]{1,0:T(8,128)(2,1)S(1)}, u32[]{:S(2)}, u32[]{:S(2)}) collective-permute-start(bf16[160,512]{1,0:T(8,128)(2,1)S(1)} %get-tuple-element.69), channel_id=1, source_target_pairs={{0,128},{32,160},{64,192},{96,224},{128,256},{160,288},{192,320},{... | collective-permute-start | bytes 491528 | tf_op jit(solution)/shard_map/ppermute | solution.py:23
  206.2 17.5 %collective-permute-start.23 = (bf16[160,512]{1,0:T(8,128)(2,1)S(1)}, bf16[160,512]{1,0:T(8,128)(2,1)S(1)}, u32[]{:S(2)}, u32[]{:S(2)}) collective-permute-start(bf16[160,512]{1,0:T(8,128)(2,1)S(1)} %get-tuple-element.70), channel_id=1, source_target_pairs={{0,384},{32,416},{64,448},{96,480},{128,0},{160,32},{192,64},{224,... | collective-permute-start | bytes 491528 | tf_op jit(solution)/shard_map/ppermute | solution.py:23
  214.8 22.5 %collective-permute-start.21 = (bf16[288,512]{1,0:T(8,128)(2,1)S(1)}, bf16[288,512]{1,0:T(8,128)(2,1)S(1)}, u32[]{:S(2)}, u32[]{:S(2)}) collective-permute-start(bf16[288,512]{1,0:T(8,128)(2,1)S(1)} %pad_maximum_fusion.2), channel_id=1, source_target_pairs={{0,128},{32,160},{64,192},{96,224},{128,256},{160,288},{192,320},{... | collective-permute-start | bytes 884744 | tf_op jit(solution)/shard_map/ppermute | solution.py:23
  223.7 26.2 %collective-permute-start.24 = (bf16[256,512]{1,0:T(8,128)(2,1)S(1)}, bf16[256,512]{1,0:T(8,128)(2,1)S(1)}, u32[]{:S(2)}, u32[]{:S(2)}) collective-permute-start(bf16[256,512]{1,0:T(8,128)(2,1)S(1)} %pad_maximum_fusion.3), channel_id=1, source_target_pairs={{0,384},{32,416},{64,448},{96,480},{128,0},{160,32},{192,64},{224,... | collective-permute-start | bytes 786440 | tf_op jit(solution)/shard_map/ppermute | solution.py:23
  (8 other events, 160.6 us)
Sparse Core Ops, SparseCore 0:
  10.1 101.3 all-gather.1

commit v3 on v2

--- a/solution.py
+++ b/solution.py
@@ -21,6 +21,11 @@
         (zh * 4 + x, ((zh + dzh) % 4) * 4 + (x + dx) % 4) for zh in range(4) for x in range(4)
     ]
     return lax.ppermute(value, "dp", pairs)
+
+
+def dp_pairs(value, offset):
+    pairs = [(i, i + 1) for i in range(offset, 15, 2)]
+    return lax.ppermute(value, "dp", pairs + [(j, i) for i, j in pairs])
 
 
 def shifted(value, steps):
@@ -50,18 +55,18 @@
 
 
 def forward_kernel(idx_ref, x_ref, taps_ref, *refs):
-    w_refs, (out_ref, prev_ref, head_ref, x_buf, w_buf, x_sem, w_sem) = refs[:8], refs[8:]
+    w_refs, (out_ref, edge_ref, x_buf, w_buf, x_sem, w_sem) = refs[:8], refs[8:]
     blocks, rows, depth = x_ref.shape
     width, half = w_buf.shape[2], rows // 2
-    for block in range(blocks):
-        pltpu.make_async_copy(
-            x_ref.at[block], x_buf.at[:, block * depth : (block + 1) * depth], x_sem.at[block]
-        ).start()
     for piece, ref in enumerate(w_refs):
         rel, first = W_PIECES[piece]
         for k in range(ref.shape[0]):
             slot = lax.rem(idx_ref[0] + ZH_REL[first + k], 4) * 4 + lax.rem(idx_ref[1] + rel, 4)
             pltpu.make_async_copy(ref.at[k], w_buf.at[slot], w_sem.at[slot]).start()
+    for block in range(blocks):
+        pltpu.make_async_copy(
+            x_ref.at[block], x_buf.at[:, block * depth : (block + 1) * depth], x_sem.at[block]
+        ).start()
     totals = [jnp.zeros((half, width), F32) for _ in range(2)]
     for part in range(4):
         for block in range(8 * part, 8 * part + 8):
@@ -77,8 +82,8 @@
                 weights,
                 preferred_element_type=F32,
             )
-    head_ref[...] = jnp.concatenate([total[:8] for total in totals]).astype(BF)
-    prev_ref[128:] = jnp.concatenate([total[half - 8 :] for total in totals]).astype(BF)
+    edge_ref[128:144] = jnp.concatenate([total[half - 8 :] for total in totals]).astype(BF)
+    edge_ref[144:160] = jnp.concatenate([total[:8] for total in totals]).astype(BF)
     for s in range(2):
         turned = totals[s].T.astype(BF)
         out_ref[:, s * half : (s + 1) * half] = turned
@@ -86,7 +91,7 @@
         for b in range(2):
             branch = slice(128 * b, 128 * b + 128)
             smooth.append(short_smooth(turned[branch].astype(F32), taps_ref, branch)[:, half - 128 :])
-        prev_ref[:128, s * 128 : (s + 1) * 128] = (smooth[0] * smooth[1]).astype(BF)
+        edge_ref[:128, s * 128 : (s + 1) * 128] = (smooth[0] * smooth[1]).astype(BF)
 
 
 def short_smooth(ext, taps_ref, rows):
@@ -103,8 +108,7 @@
         forward_kernel,
         out_shape=[
             jax.ShapeDtypeStruct((width, rows), BF),
-            jax.ShapeDtypeStruct((144, width), BF),
-            jax.ShapeDtypeStruct((16, width), BF),
+            jax.ShapeDtypeStruct((160, width), BF),
         ],
         in_specs=[
             pl.BlockSpec(memory_space=pltpu.SMEM),
@@ -112,7 +116,7 @@
             pl.BlockSpec(memory_space=pltpu.VMEM),
         ]
         + [pl.BlockSpec(memory_space=pl.ANY)] * 8,
-        out_specs=[pl.BlockSpec(memory_space=pltpu.VMEM)] * 3,
+        out_specs=[pl.BlockSpec(memory_space=pltpu.VMEM)] * 2,
         scratch_shapes=[
             pltpu.VMEM((rows, blocks * depth), BF),
             pltpu.VMEM((blocks // 2, 2 * depth, width), BF),
@@ -315,14 +319,17 @@
 
 
 def middle_kernel(
-    kv_ref, prev_ref, head_ref, grad_ref, taps_ref, dy_ref, prod_ref, sums_ref
+    meta_ref, kv_ref, first_ref, second_ref, grad_ref, taps_ref, dy_ref, prod_ref, sums_ref
 ):
     lanes = lax.broadcasted_iota(jnp.int32, (128, 128), 1)
     sums = jnp.zeros((128, 128), F32)
     partial = [[None] * 7 for _ in range(2)]
     zeros = jnp.zeros((112, 256), F32)
-    before = jnp.concatenate([prev_ref[128:].astype(F32), zeros]).T
-    after = jnp.concatenate([head_ref[...].astype(F32), zeros]).T
+    odd = meta_ref[3] == 1
+    first, second = first_ref[...].astype(F32), second_ref[...].astype(F32)
+    left, right = jnp.where(odd, first, second), jnp.where(odd, second, first)
+    before = jnp.concatenate([left[128:144], zeros]).T
+    after = jnp.concatenate([right[144:], zeros]).T
     for s in range(2):
         smooth = []
         for b in range(2):
@@ -336,7 +343,7 @@
                 axis=1,
             )
             smooth.append(short_smooth(ext, taps_ref, rows)[:, 128:])
-        prod_ref[:, s * 384 : s * 384 + 128] = prev_ref[:128, s * 128 : (s + 1) * 128]
+        prod_ref[:, s * 384 : s * 384 + 128] = left[:128, s * 128 : (s + 1) * 128].astype(BF)
         prod_ref[:, s * 384 + 128 : (s + 1) * 384] = (
             smooth[0][:, :256] * smooth[1][:, :256]
         ).astype(BF)
@@ -359,7 +366,7 @@
     sums_ref[...] = sums.T[0:16]
 
 
-def middle_terms(kv, prev, head, grad, taps):
+def middle_terms(meta, kv, first, second, grad, taps):
     return pl.pallas_call(
         middle_kernel,
         out_shape=[
@@ -367,9 +374,9 @@
             jax.ShapeDtypeStruct((128, 768), BF),
             jax.ShapeDtypeStruct((16, 128), F32),
         ],
-        in_specs=[pl.BlockSpec(memory_space=pltpu.VMEM)] * 5,
+        in_specs=[pl.BlockSpec(memory_space=pltpu.SMEM)] + [pl.BlockSpec(memory_space=pltpu.VMEM)] * 5,
         out_specs=[pl.BlockSpec(memory_space=pltpu.VMEM)] * 3,
-    )(kv, prev, head, grad, taps)
+    )(meta, kv, first, second, grad, taps)
 
 
 def response_kernel(meta_ref, prod, up_ref, band_ref, sums_ref, mixed_ref, small_ref, resp):
@@ -422,7 +429,9 @@
     channels = key_panel.shape[1]
     dp = lax.axis_index("dp")
     idx = jnp.stack([dp // 4, dp % 4]).astype(jnp.int32)
-    meta = jnp.concatenate([(dp * count).reshape(1).astype(jnp.int32), lengths])
+    meta = jnp.concatenate(
+        [(dp * count).reshape(1).astype(jnp.int32), lengths, (dp % 2).reshape(1).astype(jnp.int32)]
+    )
 
     features = lax.all_gather(inputs.reshape(seqs * count, local_width), "shard", axis=0)
     features = in_hbm(features)
@@ -431,10 +440,10 @@
     up, product_grad, bands = cotangent_terms(meta, cotangent, after, medium_filters)
 
     taps = jnp.pad(short_filters.reshape(256, 7), ((0, 0), (0, 1)))
-    kv, prev, head = forward_matmul(idx, features, taps, panels)
-    prev = in_hbm(shifted(prev, 1))
-    head = in_hbm(shifted(head, -1))
-    outgoing, product, sums = middle_terms(in_hbm(kv), prev, head, product_grad, taps)
+    kv, edges = forward_matmul(idx, features, taps, panels)
+    first = dp_pairs(edges, 0)
+    second = dp_pairs(edges, 1)
+    outgoing, product, sums = middle_terms(meta, in_hbm(kv), first, second, product_grad, taps)
     outgoing = in_hbm(outgoing)
     mixed, small = response_terms(meta, product, up, bands, sums)
     key_grad, value_grad, small = reduce_grads(idx, features, outgoing, small)

time: 260 us -> 264 us (1.015)
  the two profiles are of different devices: /device:TPU:8 before, /device:TPU:104 now
where the time goes in v3:
time: 264 us; the launch traced here: 263 us
  starting transfers between devices  125 us (47%)
  waiting for transfers between devices  77.1 us (29%)
  Pallas kernels  28.3 us (11%)
  between operations  14.6 us (6%)
  local copies, waits for them, and re-layouts  12.6 us (5%)
  other arithmetic  4.63 us (2%)
    ppermute x22, starting transfers between devices, dp_move(): return lax.ppermute(value, 'dp', pairs)  120 us
    ppermute x22, waiting for transfers between devices, dp_move(): return lax.ppermute(value, 'dp', pairs)  69.3 us
    pallas_call x2, Pallas kernels, backward_matmul(): pl.pallas_call(functools.partial(backward_kernel, rels), out_shape=[sent,...  9.06 us
    pallas_call x1, Pallas kernels, forward_matmul(): pl.pallas_call(forward_kernel, out_shape=[jax.ShapeDtypeStruct((width, ro...  7.69 us
    all_gather x1, waiting for transfers between devices, body(): lax.all_gather(inputs.reshape(seqs * count, local_width), 'shard', axis=0)  7.11 us
    pallas_call x1, Pallas kernels, middle_terms(): pl.pallas_call(middle_kernel, out_shape=[jax.ShapeDtypeStruct((256, 512),...  6.28 us
    unnamed x17, local copies, waits for them, and re-layouts  5.89 us
  transfers between devices with their start and end apart: 26, of which 11 were waited for; matrix products, arithmetic and copies ran while one was open for 5% of the time, Pallas kernels for 6%

profile of v3, /device:TPU:104, one launch (start us, length us, event | category | flops | bytes accessed | tf_op | source)
XLA Modules:
  0.0 262.7 jit_solution(11909586226169107649)
XLA Ops:
  9.8 9.1 %collective-permute-start = (bf16[512,256]{1,0:T(8,128)(2,1)S(1)}, bf16[512,256]{1,0:T(8,128)(2,1)S(1)}, u32[]{:S(2)}, u32[]{:S(2)}) collective-permute-start(bf16[512,256]{1,0:T(8,128)(2,1)S(1)} %constant_dynamic-update-slice_fusion), channel_id=1, source_target_pairs={{0,128},{32,160},{64,192},{96,224},{128,256},{160,288},{192,320},{... | collective-permute-start | bytes 786440 | tf_op jit(solution)/shard_map/ppermute | solution.py:23
  21.7 21.2 %collective-permute-done = bf16[512,256]{1,0:T(8,128)(2,1)S(1)} collective-permute-done((bf16[512,256]{1,0:T(8,128)(2,1)S(1)}, bf16[512,256]{1,0:T(8,128)(2,1)S(1)}, u32[]{:S(2)}, u32[]{:S(2)}) %collective-permute-start) | collective-permute-done | bytes 262176 | tf_op jit(solution)/shard_map/ppermute | solution.py:23
  43.1 4.7 %collective-permute-start.6 = (bf16[3,512,256]{2,1,0:T(8,128)(2,1)S(1)}, bf16[3,512,256]{2,1,0:T(8,128)(2,1)S(1)}, u32[]{:S(2)}, u32[]{:S(2)}) collective-permute-start(bf16[3,512,256]{2,1,0:T(8,128)(2,1)S(1)} %pad_maximum_fusion.refs_0_), channel_id=1, source_target_pairs={{0,96},{32,0},{64,32},{96,64},{128,224},{160,128},{192,160},{224,1... | collective-permute-start | bytes 2359304 | tf_op jit(solution)/shard_map/ppermute | solution.py:23
  49.7 5.2 %collective-permute-start.2 = (bf16[256,256]{1,0:T(8,128)(2,1)S(1)}, bf16[256,256]{1,0:T(8,128)(2,1)S(1)}, u32[]{:S(2)}, u32[]{:S(2)}) collective-permute-start(bf16[256,256]{1,0:T(8,128)(2,1)S(1)} %slice.220), channel_id=1, source_target_pairs={{0,128},{32,160},{64,192},{96,224},{128,256},{160,288},{192,320},{... | collective-permute-start | bytes 393224 | tf_op jit(solution)/shard_map/ppermute | solution.py:23
  54.9 4.5 %collective-permute-start.3 = (bf16[256,256]{1,0:T(8,128)(2,1)S(1)}, bf16[256,256]{1,0:T(8,128)(2,1)S(1)}, u32[]{:S(2)}, u32[]{:S(2)}) collective-permute-start(bf16[256,256]{1,0:T(8,128)(2,1)S(1)} %slice.221), channel_id=1, source_target_pairs={{0,384},{32,416},{64,448},{96,480},{128,0},{160,32},{192,64},{224,... | collective-permute-start | bytes 393224 | tf_op jit(solution)/shard_map/ppermute | solution.py:23
  61.0 4.7 %collective-permute-done.3 = bf16[256,256]{1,0:T(8,128)(2,1)S(1)} collective-permute-done((bf16[256,256]{1,0:T(8,128)(2,1)S(1)}, bf16[256,256]{1,0:T(8,128)(2,1)S(1)}, u32[]{:S(2)}, u32[]{:S(2)}) %collective-permute-start.3) | collective-permute-done | bytes 131104 | tf_op jit(solution)/shard_map/ppermute | solution.py:23
  65.7 5.1 %collective-permute-start.7 = (bf16[1,512,256]{2,1,0:T(8,128)(2,1)S(1)}, bf16[1,512,256]{2,1,0:T(8,128)(2,1)S(1)}, u32[]{:S(2)}, u32[]{:S(2)}) collective-permute-start(bf16[1,512,256]{2,1,0:T(8,128)(2,1)S(1)} %maximum_bitcast_fusion.refs_1_), channel_id=1, source_target_pairs={{0,96},{32,0},{64,32},{96,64},{128,224},{160,128},{192,160},{224,1... | collective-permute-start | bytes 786440 | tf_op jit(solution)/shard_map/ppermute | solution.py:23
  75.6 5.6 %collective-permute-start.9 = (bf16[2,512,256]{2,1,0:T(8,128)(2,1)}, bf16[2,512,256]{2,1,0:T(8,128)(2,1)S(1)}, u32[]{:S(2)}, u32[]{:S(2)}) collective-permute-start(bf16[2,512,256]{2,1,0:T(8,128)(2,1)} %pad_maximum_fusion.1), channel_id=1, source_target_pairs={{0,96},{32,0},{64,32},{96,64},{128,224},{160,128},{192,160},{224,1... | collective-permute-start | bytes 1572872 | tf_op jit(solution)/shard_map/ppermute | solution.py:23
  86.8 4.6 %collective-permute-start.5 = (bf16[1,512,256]{2,1,0:T(8,128)(2,1)S(1)}, bf16[1,512,256]{2,1,0:T(8,128)(2,1)}, u32[]{:S(2)}, u32[]{:S(2)}) collective-permute-start(bf16[1,512,256]{2,1,0:T(8,128)(2,1)S(1)} %maximum_bitcast_fusion.refs_1_), channel_id=1, source_target_pairs={{0,32},{32,64},{64,96},{96,0},{128,160},{160,192},{192,224},{224,1... | collective-permute-start | bytes 786440 | tf_op jit(solution)/shard_map/ppermute | solution.py:23
  97.4 4.1 %collective-permute-done.5.refs_3_ = bf16[1,512,256]{2,1,0:T(8,128)(2,1)} collective-permute-done((bf16[1,512,256]{2,1,0:T(8,128)(2,1)S(1)}, bf16[1,512,256]{2,1,0:T(8,128)(2,1)}, u32[]{:S(2)}, u32[]{:S(2)}) %collective-permute-start.5) | collective-permute-done | bytes 262176 | tf_op jit(solution)/shard_map/ppermute | solution.py:23
  101.5 7.1 %all-gather.2.cloned.1.call-done.x_ref = bf16[32,512,256]{2,1,0:T(8,128)(2,1)} async-done(((bf16[1,512,256]{2,1,0:T(8,128)(2,1)}), bf16[32,512,256]{2,1,0:T(8,128)(2,1)}) %all-gather.2.cloned.1.call-update) | async-done | bytes 8388624 | tf_op jit(solution)/shard_map/all_gather | solution.py:436
  108.6 7.7 %shard_map.110 = (bf16[256,512]{1,0:T(8,128)(2,1)S(1)}, bf16[160,256]{1,0:T(8,128)(2,1)}) custom-call(s32[2]{0:T(128)S(1)} %pad_add_fusion.1.idx_ref, bf16[32,512,256]{2,1,0:T(8,128)(2,1)} %all-gather.2.cloned.1.call-done.x_ref, f32[256,8]{1,0:T(8,128)S(1)} %pad.5.taps_ref, bf16[3,512,256]{2,1,0:T(8,128)(2,1)S(1)} %pad_maximum_fusion.refs_0_, ...), custom_call_target="tpu_custom_call" | custom-call | tf_op jit(solution)/shard_map/pallas_call | solution.py:107
  124.7 6.3 %shard_map.112 = (bf16[256,512]{1,0:T(8,128)(2,1)}, bf16[128,768]{1,0:T(8,128)(2,1)}, f32[16,128]{1,0:T(8,128)}) custom-call(s32[4]{0:T(128)} %pad_add_fusion.meta_ref, bf16[256,512]{1,0:T(8,128)(2,1)} %copy-done.1, bf16[160,256]{1,0:T(8,128)(2,1)} %copy-done.2, bf16[160,256]{1,0:T(8,128)(2,1)} %copy-done.3, f32[128,768]{1,0:T(8,128)} %get-tuple-element.29.grad_ref, ...), custom_call_target="tpu_custom_call" | custom-call | tf_op jit(solution)/shard_map/pallas_call | solution.py:370
  137.1 6.1 %collective-permute-start.16 = (bf16[288,512]{1,0:T(8,128)(2,1)S(1)}, bf16[288,512]{1,0:T(8,128)(2,1)S(1)}, u32[]{:S(2)}, u32[]{:S(2)}) collective-permute-start(bf16[288,512]{1,0:T(8,128)(2,1)S(1)} %get-tuple-element.42), channel_id=1, source_target_pairs={{0,32},{32,64},{64,96},{96,0},{128,160},{160,192},{192,224},{224,1... | collective-permute-start | bytes 884744 | tf_op jit(solution)/shard_map/ppermute | solution.py:23
  143.2 8.8 %collective-permute-start.17 = (bf16[288,512]{1,0:T(8,128)(2,1)S(1)}, bf16[288,512]{1,0:T(8,128)(2,1)S(1)}, u32[]{:S(2)}, u32[]{:S(2)}) collective-permute-start(bf16[288,512]{1,0:T(8,128)(2,1)S(1)} %get-tuple-element.43), channel_id=1, source_target_pairs={{0,96},{32,0},{64,32},{96,64},{128,224},{160,128},{192,160},{224,1... | collective-permute-start | bytes 884744 | tf_op jit(solution)/shard_map/ppermute | solution.py:23
  152.0 5.8 %shard_map.114 = (bf16[768,512]{1,0:T(8,128)(2,1)S(1)}, bf16[768,512]{1,0:T(8,128)(2,1)S(1)}, bf16[384,512]{1,0:T(8,128)(2,1)S(1)}, bf16[384,512]{1,0:T(8,128)(2,1)S(1)}, bf16[768,512]{1,0:T(8,128)(2,1)S(1)}) custom-call(s32[2]{0:T(128)S(1)} %pad_add_fusion.1.idx_ref, bf16[32,512,256]{2,1,0:T(8,128)(2,1)} %all-gather.2.cloned.1.call-done.x_ref, ...), custom_call_target="tpu_custom_call" | custom-call | tf_op jit(solution)/shard_map/pallas_call | solution.py:199
  159.8 5.1 %collective-permute-start.13 = (bf16[768,512]{1,0:T(8,128)(2,1)S(1)}, bf16[768,512]{1,0:T(8,128)(2,1)S(1)}, u32[]{:S(2)}, u32[]{:S(2)}) collective-permute-start(bf16[768,512]{1,0:T(8,128)(2,1)S(1)} %get-tuple-element.37), channel_id=1, source_target_pairs={{0,96},{32,0},{64,32},{96,64},{128,224},{160,128},{192,160},{224,1... | collective-permute-start | bytes 2359304 | tf_op jit(solution)/shard_map/ppermute | solution.py:23
  167.0 5.1 %collective-permute-start.22 = (bf16[128,512]{1,0:T(8,128)(2,1)S(1)}, bf16[128,512]{1,0:T(8,128)(2,1)S(1)}, u32[]{:S(2)}, u32[]{:S(2)}) collective-permute-start(bf16[128,512]{1,0:T(8,128)(2,1)S(1)} %add_convert_fusion.3), channel_id=1, source_target_pairs={{0,96},{32,0},{64,32},{96,64},{128,224},{160,128},{192,160},{224,1... | collective-permute-start | bytes 393224 | tf_op jit(solution)/shard_map/ppermute | solution.py:23
  172.1 10.4 %collective-permute-done.18 = bf16[160,512]{1,0:T(8,128)(2,1)S(1)} collective-permute-done((bf16[160,512]{1,0:T(8,128)(2,1)S(1)}, bf16[160,512]{1,0:T(8,128)(2,1)S(1)}, u32[]{:S(2)}, u32[]{:S(2)}) %collective-permute-start.18) | collective-permute-done | bytes 163872 | tf_op jit(solution)/shard_map/ppermute | solution.py:23
  185.9 4.9 %collective-permute-start.20 = (bf16[384,512]{1,0:T(8,128)(2,1)S(1)}, bf16[384,512]{1,0:T(8,128)(2,1)S(1)}, u32[]{:S(2)}, u32[]{:S(2)}) collective-permute-start(bf16[384,512]{1,0:T(8,128)(2,1)S(1)} %add_convert_fusion), channel_id=1, source_target_pairs={{0,96},{32,0},{64,32},{96,64},{128,224},{160,128},{192,160},{224,1... | collective-permute-start | bytes 1179656 | tf_op jit(solution)/shard_map/ppermute | solution.py:23
  191.0 7.1 %collective-permute-start.19 = (bf16[160,512]{1,0:T(8,128)(2,1)S(1)}, bf16[160,512]{1,0:T(8,128)(2,1)S(1)}, u32[]{:S(2)}, u32[]{:S(2)}) collective-permute-start(bf16[160,512]{1,0:T(8,128)(2,1)S(1)} %get-tuple-element.67), channel_id=1, source_target_pairs={{0,128},{32,160},{64,192},{96,224},{128,256},{160,288},{192,320},{... | collective-permute-start | bytes 491528 | tf_op jit(solution)/shard_map/ppermute | solution.py:23
  200.7 11.5 %collective-permute-done.19 = bf16[160,512]{1,0:T(8,128)(2,1)S(1)} collective-permute-done((bf16[160,512]{1,0:T(8,128)(2,1)S(1)}, bf16[160,512]{1,0:T(8,128)(2,1)S(1)}, u32[]{:S(2)}, u32[]{:S(2)}) %collective-permute-start.19) | collective-permute-done | bytes 163872 | tf_op jit(solution)/shard_map/ppermute | solution.py:23
  212.7 26.6 %collective-permute-start.21 = (bf16[288,512]{1,0:T(8,128)(2,1)S(1)}, bf16[288,512]{1,0:T(8,128)(2,1)S(1)}, u32[]{:S(2)}, u32[]{:S(2)}) collective-permute-start(bf16[288,512]{1,0:T(8,128)(2,1)S(1)} %pad_maximum_fusion.2), channel_id=1, source_target_pairs={{0,128},{32,160},{64,192},{96,224},{128,256},{160,288},{192,320},{... | collective-permute-start | bytes 884744 | tf_op jit(solution)/shard_map/ppermute | solution.py:23
  245.3 8.2 %collective-permute-done.24 = bf16[256,512]{1,0:T(8,128)(2,1)S(1)} collective-permute-done((bf16[256,512]{1,0:T(8,128)(2,1)S(1)}, bf16[256,512]{1,0:T(8,128)(2,1)S(1)}, u32[]{:S(2)}, u32[]{:S(2)}) %collective-permute-start.24) | collective-permute-done | bytes 262176 | tf_op jit(solution)/shard_map/ppermute | solution.py:23
  (96 shorter events, 58.4 us)
Async XLA Ops:
  7.2 101.5 %all-gather.2.cloned.1.call-start = ((), (), s32[]{:S(2)}) async-start(), calls=%async_computation | async-start | bytes 8650752 | tf_op jit(solution)/shard_map/all_gather | solution.py:436
  9.8 33.2 %collective-permute-start = (bf16[512,256]{1,0:T(8,128)(2,1)S(1)}, bf16[512,256]{1,0:T(8,128)(2,1)S(1)}, u32[]{:S(2)}, u32[]{:S(2)}) collective-permute-start(bf16[512,256]{1,0:T(8,128)(2,1)S(1)} %constant_dynamic-update-slice_fusion), channel_id=1, source_target_pairs={{0,128},{32,160},{64,192},{96,224},{128,256},{160,288},{192,320},{... | collective-permute-start | bytes 786440 | tf_op jit(solution)/shard_map/ppermute | solution.py:23
  18.9 24.1 %collective-permute-start.1 = (bf16[512,256]{1,0:T(8,128)(2,1)S(1)}, bf16[512,256]{1,0:T(8,128)(2,1)S(1)}, u32[]{:S(2)}, u32[]{:S(2)}) collective-permute-start(bf16[512,256]{1,0:T(8,128)(2,1)S(1)} %constant_dynamic-update-slice_fusion), channel_id=1, source_target_pairs={{0,384},{32,416},{64,448},{96,480},{128,0},{160,32},{192,64},{224,... | collective-permute-start | bytes 786440 | tf_op jit(solution)/shard_map/ppermute | solution.py:23
  43.1 27.8 %collective-permute-start.6 = (bf16[3,512,256]{2,1,0:T(8,128)(2,1)S(1)}, bf16[3,512,256]{2,1,0:T(8,128)(2,1)S(1)}, u32[]{:S(2)}, u32[]{:S(2)}) collective-permute-start(bf16[3,512,256]{2,1,0:T(8,128)(2,1)S(1)} %pad_maximum_fusion.refs_0_), channel_id=1, source_target_pairs={{0,96},{32,0},{64,32},{96,64},{128,224},{160,128},{192,160},{224,1... | collective-permute-start | bytes 2359304 | tf_op jit(solution)/shard_map/ppermute | solution.py:23
  47.7 33.5 %collective-permute-start.4 = (bf16[3,512,256]{2,1,0:T(8,128)(2,1)S(1)}, bf16[3,512,256]{2,1,0:T(8,128)(2,1)S(1)}, u32[]{:S(2)}, u32[]{:S(2)}) collective-permute-start(bf16[3,512,256]{2,1,0:T(8,128)(2,1)S(1)} %pad_maximum_fusion.refs_0_), channel_id=1, source_target_pairs={{0,32},{32,64},{64,96},{96,0},{128,160},{160,192},{192,224},{224,1... | collective-permute-start | bytes 2359304 | tf_op jit(solution)/shard_map/ppermute | solution.py:23
  49.7 11.3 %collective-permute-start.2 = (bf16[256,256]{1,0:T(8,128)(2,1)S(1)}, bf16[256,256]{1,0:T(8,128)(2,1)S(1)}, u32[]{:S(2)}, u32[]{:S(2)}) collective-permute-start(bf16[256,256]{1,0:T(8,128)(2,1)S(1)} %slice.220), channel_id=1, source_target_pairs={{0,128},{32,160},{64,192},{96,224},{128,256},{160,288},{192,320},{... | collective-permute-start | bytes 393224 | tf_op jit(solution)/shard_map/ppermute | solution.py:23
  54.9 10.8 %collective-permute-start.3 = (bf16[256,256]{1,0:T(8,128)(2,1)S(1)}, bf16[256,256]{1,0:T(8,128)(2,1)S(1)}, u32[]{:S(2)}, u32[]{:S(2)}) collective-permute-start(bf16[256,256]{1,0:T(8,128)(2,1)S(1)} %slice.221), channel_id=1, source_target_pairs={{0,384},{32,416},{64,448},{96,480},{128,0},{160,32},{192,64},{224,... | collective-permute-start | bytes 393224 | tf_op jit(solution)/shard_map/ppermute | solution.py:23
  65.7 9.0 %collective-permute-start.7 = (bf16[1,512,256]{2,1,0:T(8,128)(2,1)S(1)}, bf16[1,512,256]{2,1,0:T(8,128)(2,1)S(1)}, u32[]{:S(2)}, u32[]{:S(2)}) collective-permute-start(bf16[1,512,256]{2,1,0:T(8,128)(2,1)S(1)} %maximum_bitcast_fusion.refs_1_), channel_id=1, source_target_pairs={{0,96},{32,0},{64,32},{96,64},{128,224},{160,128},{192,160},{224,1... | collective-permute-start | bytes 786440 | tf_op jit(solution)/shard_map/ppermute | solution.py:23
  75.6 25.9 %collective-permute-start.9 = (bf16[2,512,256]{2,1,0:T(8,128)(2,1)}, bf16[2,512,256]{2,1,0:T(8,128)(2,1)S(1)}, u32[]{:S(2)}, u32[]{:S(2)}) collective-permute-start(bf16[2,512,256]{2,1,0:T(8,128)(2,1)} %pad_maximum_fusion.1), channel_id=1, source_target_pairs={{0,96},{32,0},{64,32},{96,64},{128,224},{160,128},{192,160},{224,1... | collective-permute-start | bytes 1572872 | tf_op jit(solution)/shard_map/ppermute | solution.py:23
  82.1 19.5 %collective-permute-start.8 = (bf16[2,512,256]{2,1,0:T(8,128)(2,1)}, bf16[2,512,256]{2,1,0:T(8,128)(2,1)}, u32[]{:S(2)}, u32[]{:S(2)}) collective-permute-start(bf16[2,512,256]{2,1,0:T(8,128)(2,1)} %slice.222), channel_id=1, source_target_pairs={{0,32},{32,64},{64,96},{96,0},{128,160},{160,192},{192,224},{224,1... | collective-permute-start | bytes 1572872 | tf_op jit(solution)/shard_map/ppermute | solution.py:23
  85.5 36.1 %collective-permute-start.12 = (bf16[2,144,128]{2,1,0:T(8,128)(2,1)}, bf16[2,144,128]{2,1,0:T(8,128)(2,1)}, u32[]{:S(2)}, u32[]{:S(2)}) collective-permute-start(bf16[2,144,128]{2,1,0:T(8,128)(2,1)} %slice.174), channel_id=1, source_target_pairs={{32,0},{64,32},{96,64},{128,96},{160,128},{192,160},{224,192},{256... | collective-permute-start | bytes 221192 | tf_op jit(solution)/shard_map/ppermute | solution.py:33
  86.8 14.7 %collective-permute-start.5 = (bf16[1,512,256]{2,1,0:T(8,128)(2,1)S(1)}, bf16[1,512,256]{2,1,0:T(8,128)(2,1)}, u32[]{:S(2)}, u32[]{:S(2)}) collective-permute-start(bf16[1,512,256]{2,1,0:T(8,128)(2,1)S(1)} %maximum_bitcast_fusion.refs_1_), channel_id=1, source_target_pairs={{0,32},{32,64},{64,96},{96,0},{128,160},{160,192},{192,224},{224,1... | collective-permute-start | bytes 786440 | tf_op jit(solution)/shard_map/ppermute | solution.py:23
  137.1 27.8 %collective-permute-start.16 = (bf16[288,512]{1,0:T(8,128)(2,1)S(1)}, bf16[288,512]{1,0:T(8,128)(2,1)S(1)}, u32[]{:S(2)}, u32[]{:S(2)}) collective-permute-start(bf16[288,512]{1,0:T(8,128)(2,1)S(1)} %get-tuple-element.42), channel_id=1, source_target_pairs={{0,32},{32,64},{64,96},{96,0},{128,160},{160,192},{192,224},{224,1... | collective-permute-start | bytes 884744 | tf_op jit(solution)/shard_map/ppermute | solution.py:23
  143.2 23.7 %collective-permute-start.17 = (bf16[288,512]{1,0:T(8,128)(2,1)S(1)}, bf16[288,512]{1,0:T(8,128)(2,1)S(1)}, u32[]{:S(2)}, u32[]{:S(2)}) collective-permute-start(bf16[288,512]{1,0:T(8,128)(2,1)S(1)} %get-tuple-element.43), channel_id=1, source_target_pairs={{0,96},{32,0},{64,32},{96,64},{128,224},{160,128},{192,160},{224,1... | collective-permute-start | bytes 884744 | tf_op jit(solution)/shard_map/ppermute | solution.py:23
  157.8 25.3 %collective-permute-start.14 = (bf16[768,512]{1,0:T(8,128)(2,1)S(1)}, bf16[768,512]{1,0:T(8,128)(2,1)S(1)}, u32[]{:S(2)}, u32[]{:S(2)}) collective-permute-start(bf16[768,512]{1,0:T(8,128)(2,1)S(1)} %get-tuple-element.39), channel_id=1, source_target_pairs={{0,32},{32,64},{64,96},{96,0},{128,160},{160,192},{192,224},{224,1... | collective-permute-start | bytes 2359304 | tf_op jit(solution)/shard_map/ppermute | solution.py:23
  159.8 26.1 %collective-permute-start.13 = (bf16[768,512]{1,0:T(8,128)(2,1)S(1)}, bf16[768,512]{1,0:T(8,128)(2,1)S(1)}, u32[]{:S(2)}, u32[]{:S(2)}) collective-permute-start(bf16[768,512]{1,0:T(8,128)(2,1)S(1)} %get-tuple-element.37), channel_id=1, source_target_pairs={{0,96},{32,0},{64,32},{96,64},{128,224},{160,128},{192,160},{224,1... | collective-permute-start | bytes 2359304 | tf_op jit(solution)/shard_map/ppermute | solution.py:23
  165.0 17.6 %collective-permute-start.18 = (bf16[160,512]{1,0:T(8,128)(2,1)S(1)}, bf16[160,512]{1,0:T(8,128)(2,1)S(1)}, u32[]{:S(2)}, u32[]{:S(2)}) collective-permute-start(bf16[160,512]{1,0:T(8,128)(2,1)S(1)} %pad_maximum_fusion.4), channel_id=1, source_target_pairs={{0,32},{32,64},{64,96},{96,0},{128,160},{160,192},{192,224},{224,1... | collective-permute-start | bytes 491528 | tf_op jit(solution)/shard_map/ppermute | solution.py:23
  167.0 16.1 %collective-permute-start.22 = (bf16[128,512]{1,0:T(8,128)(2,1)S(1)}, bf16[128,512]{1,0:T(8,128)(2,1)S(1)}, u32[]{:S(2)}, u32[]{:S(2)}) collective-permute-start(bf16[128,512]{1,0:T(8,128)(2,1)S(1)} %add_convert_fusion.3), channel_id=1, source_target_pairs={{0,96},{32,0},{64,32},{96,64},{128,224},{160,128},{192,160},{224,1... | collective-permute-start | bytes 393224 | tf_op jit(solution)/shard_map/ppermute | solution.py:23
  183.2 29.0 %collective-permute-start.15 = (bf16[384,512]{1,0:T(8,128)(2,1)S(1)}, bf16[384,512]{1,0:T(8,128)(2,1)S(1)}, u32[]{:S(2)}, u32[]{:S(2)}) collective-permute-start(bf16[384,512]{1,0:T(8,128)(2,1)S(1)} %add_convert_fusion.1), channel_id=1, source_target_pairs={{0,32},{32,64},{64,96},{96,0},{128,160},{160,192},{192,224},{224,1... | collective-permute-start | bytes 1179656 | tf_op jit(solution)/shard_map/ppermute | solution.py:23
  185.9 26.3 %collective-permute-start.20 = (bf16[384,512]{1,0:T(8,128)(2,1)S(1)}, bf16[384,512]{1,0:T(8,128)(2,1)S(1)}, u32[]{:S(2)}, u32[]{:S(2)}) collective-permute-start(bf16[384,512]{1,0:T(8,128)(2,1)S(1)} %add_convert_fusion), channel_id=1, source_target_pairs={{0,96},{32,0},{64,32},{96,64},{128,224},{160,128},{192,160},{224,1... | collective-permute-start | bytes 1179656 | tf_op jit(solution)/shard_map/ppermute | solution.py:23
  191.0 21.3 %collective-permute-start.19 = (bf16[160,512]{1,0:T(8,128)(2,1)S(1)}, bf16[160,512]{1,0:T(8,128)(2,1)S(1)}, u32[]{:S(2)}, u32[]{:S(2)}) collective-permute-start(bf16[160,512]{1,0:T(8,128)(2,1)S(1)} %get-tuple-element.67), channel_id=1, source_target_pairs={{0,128},{32,160},{64,192},{96,224},{128,256},{160,288},{192,320},{... | collective-permute-start | bytes 491528 | tf_op jit(solution)/shard_map/ppermute | solution.py:23
  198.1 41.3 %collective-permute-start.23 = (bf16[160,512]{1,0:T(8,128)(2,1)S(1)}, bf16[160,512]{1,0:T(8,128)(2,1)S(1)}, u32[]{:S(2)}, u32[]{:S(2)}) collective-permute-start(bf16[160,512]{1,0:T(8,128)(2,1)S(1)} %get-tuple-element.68), channel_id=1, source_target_pairs={{0,384},{32,416},{64,448},{96,480},{128,0},{160,32},{192,64},{224,... | collective-permute-start | bytes 491528 | tf_op jit(solution)/shard_map/ppermute | solution.py:23
  212.7 31.9 %collective-permute-start.21 = (bf16[288,512]{1,0:T(8,128)(2,1)S(1)}, bf16[288,512]{1,0:T(8,128)(2,1)S(1)}, u32[]{:S(2)}, u32[]{:S(2)}) collective-permute-start(bf16[288,512]{1,0:T(8,128)(2,1)S(1)} %pad_maximum_fusion.2), channel_id=1, source_target_pairs={{0,128},{32,160},{64,192},{96,224},{128,256},{160,288},{192,320},{... | collective-permute-start | bytes 884744 | tf_op jit(solution)/shard_map/ppermute | solution.py:23
  239.4 14.1 %collective-permute-start.24 = (bf16[256,512]{1,0:T(8,128)(2,1)S(1)}, bf16[256,512]{1,0:T(8,128)(2,1)S(1)}, u32[]{:S(2)}, u32[]{:S(2)}) collective-permute-start(bf16[256,512]{1,0:T(8,128)(2,1)S(1)} %pad_maximum_fusion.3), channel_id=1, source_target_pairs={{0,384},{32,416},{64,448},{96,480},{128,0},{160,32},{192,64},{224,... | collective-permute-start | bytes 786440 | tf_op jit(solution)/shard_map/ppermute | solution.py:23
  (8 other events, 161.0 us)
Sparse Core Ops, SparseCore 0:
  10.1 98.4 all-gather.1

commit v4 on v3

--- a/solution.py
+++ b/solution.py
@@ -129,7 +129,7 @@
 
 GROUPS = ((2,), (1, 3, 0))
 HALF = 128
-SMALL = 32
+SMALL = 16
 
 
 def split(value):
@@ -137,15 +137,21 @@
     return high, (value - high.astype(F32)).astype(BF)
 
 
+def narrow(rows):
+    return jnp.concatenate([rows[:, 128 * q : 128 * q + 128] for q in range(4)]).astype(F32)
+
+
+def wide(value):
+    return jnp.concatenate([value[8 * q : 8 * q + 8] for q in range(4)], axis=1)
+
+
 def joined(message):
-    return message[:, :128].astype(F32) + message[:, 128:256].astype(F32)
+    return narrow(message[:8]) + narrow(message[8:])
 
 
 def put_small(ref, first, value):
-    high, rest = split(value)
-    ref[first : first + SMALL, 0:128] = high
-    ref[first : first + SMALL, 128:256] = rest
-    ref[first : first + SMALL, 256:512] = jnp.zeros((SMALL, 256), BF)
+    high = value.astype(BF).astype(F32)
+    ref[first : first + SMALL] = jnp.concatenate([wide(high), wide(value - high)]).astype(BF)
 
 
 def ring_sum(own, before, after, opposite):
@@ -154,7 +160,7 @@
 
 
 def small_rows(value):
-    return jnp.concatenate([*split(value), jnp.zeros((SMALL, 256), BF)], axis=1)
+    return jnp.concatenate([wide(part) for part in split(value)])
 
 
 def backward_kernel(rels, idx_ref, x_ref, grad_ref, *refs):
@@ -379,25 +385,25 @@
     )(meta, kv, first, second, grad, taps)
 
 
-def response_kernel(meta_ref, prod, up_ref, band_ref, sums_ref, mixed_ref, small_ref, resp):
+def product_rows(prod, rows):
+    return jnp.concatenate(
+        [
+            prod[rows, s * 384 + 128 * b : s * 384 + 128 * b + 256]
+            for s in range(2)
+            for b in range(2)
+        ]
+    )
+
+
+def correlation_kernel(prod, up_ref, sums_ref, small_ref):
     small_ref[0:16] = sums_ref[...]
     for g in range(8):
         rows = slice(16 * g, 16 * g + 16)
-        left = jnp.concatenate(
-            [
-                prod[rows, s * 384 + 128 * b : s * 384 + 128 * b + 256]
-                for s in range(2)
-                for b in range(2)
-            ]
-        )
-        total = jnp.dot(left, band_ref[g], preferred_element_type=F32)
-        for part in range(4):
-            resp[rows, part * 128 : part * 128 + 128] = total[part * 16 : part * 16 + 16]
         above = jnp.concatenate(
             [up_ref[rows, part * 128 : part * 128 + 128] for part in range(4)]
         )
         folded = lax.dot_general(
-            above, left, (((0,), (0,)), ((), ())), preferred_element_type=F32
+            above, product_rows(prod, rows), (((0,), (0,)), ((), ())), preferred_element_type=F32
         )
         count = 64
         while count >= 1:
@@ -405,23 +411,37 @@
             count //= 2
         small_ref[16 + g : 17 + g] = folded[:, :128]
         small_ref[24 + g : 25 + g] = folded[:, 128:]
+
+
+def correlation_terms(prod, up, sums):
+    return pl.pallas_call(
+        correlation_kernel,
+        out_shape=jax.ShapeDtypeStruct((32, 128), F32),
+        in_specs=[pl.BlockSpec(memory_space=pltpu.VMEM)] * 3,
+        out_specs=pl.BlockSpec(memory_space=pltpu.VMEM),
+    )(prod, up, sums)
+
+
+def response_kernel(meta_ref, prod, band_ref, mixed_ref, resp):
+    for g in range(8):
+        rows = slice(16 * g, 16 * g + 16)
+        total = jnp.dot(product_rows(prod, rows), band_ref[g], preferred_element_type=F32)
+        for part in range(4):
+            resp[rows, part * 128 : part * 128 + 128] = total[part * 16 : part * 16 + 16]
     for s in range(2):
         place = lax.broadcasted_iota(jnp.int32, (256, 128), 0) + meta_ref[0]
         turned = resp[:, s * 256 : (s + 1) * 256].T
         mixed_ref[s] = jnp.where(place < meta_ref[1 + s], turned, 0.0).astype(BF)
 
 
-def response_terms(meta, prod, up, bands, sums):
+def response_terms(meta, prod, bands):
     return pl.pallas_call(
         response_kernel,
-        out_shape=[
-            jax.ShapeDtypeStruct((2, 256, 128), BF),
-            jax.ShapeDtypeStruct((32, 128), F32),
-        ],
-        in_specs=[pl.BlockSpec(memory_space=pltpu.SMEM)] + [pl.BlockSpec(memory_space=pltpu.VMEM)] * 4,
-        out_specs=[pl.BlockSpec(memory_space=pltpu.VMEM)] * 2,
+        out_shape=jax.ShapeDtypeStruct((2, 256, 128), BF),
+        in_specs=[pl.BlockSpec(memory_space=pltpu.SMEM)] + [pl.BlockSpec(memory_space=pltpu.VMEM)] * 2,
+        out_specs=pl.BlockSpec(memory_space=pltpu.VMEM),
         scratch_shapes=[pltpu.VMEM((128, 512), F32)],
-    )(meta, prod, up, bands, sums)
+    )(meta, prod, bands)
 
 
 def body(inputs, key_panel, value_panel, short_filters, medium_filters, lengths, cotangent):
@@ -445,7 +465,8 @@
     second = dp_pairs(edges, 1)
     outgoing, product, sums = middle_terms(meta, in_hbm(kv), first, second, product_grad, taps)
     outgoing = in_hbm(outgoing)
-    mixed, small = response_terms(meta, product, up, bands, sums)
+    small = correlation_terms(product, up, sums)
+    mixed = response_terms(meta, product, bands)
     key_grad, value_grad, small = reduce_grads(idx, features, outgoing, small)
     short_grad = small[:16].reshape(2, 8, channels)[:, :7].transpose(0, 2, 1)
     medium_grad = jnp.concatenate([small[24:, :1], small[16:24, :0:-1]], axis=1)

time: 264 us -> 270 us (1.023)
  the two profiles are of different devices: /device:TPU:104 before, /device:TPU:23 now
where the time goes in v4:
time: 270 us; the launch traced here: 269 us
  waiting for transfers between devices  112 us (41%)
  starting transfers between devices  91.4 us (34%)
  Pallas kernels  30 us (11%)
  between operations  14.6 us (5%)
  local copies, waits for them, and re-layouts  12.6 us (5%)
  other arithmetic  8.32 us (3%)
    ppermute x22, waiting for transfers between devices, dp_move(): return lax.ppermute(value, 'dp', pairs)  104 us
    ppermute x22, starting transfers between devices, dp_move(): return lax.ppermute(value, 'dp', pairs)  81 us
    pallas_call x2, Pallas kernels, backward_matmul(): pl.pallas_call(functools.partial(backward_kernel, rels), out_shape=[sent,...  9.06 us
    ppermute x2, starting transfers between devices, dp_pairs(): return lax.ppermute(value, 'dp', pairs + [(j, i) for i, j in pairs])  8.41 us
    pallas_call x1, Pallas kernels, forward_matmul(): pl.pallas_call(forward_kernel, out_shape=[jax.ShapeDtypeStruct((width, ro...  7.7 us
    ppermute x2, waiting for transfers between devices, dp_pairs(): return lax.ppermute(value, 'dp', pairs + [(j, i) for i, j in pairs])  7.25 us
    pallas_call x1, Pallas kernels, middle_terms(): pl.pallas_call(middle_kernel, out_shape=[jax.ShapeDtypeStruct((256, 512),...  6.28 us
    unnamed x17, local copies, waits for them, and re-layouts  5.88 us
  transfers between devices with their start and end apart: 26, of which 14 were waited for; matrix products, arithmetic and copies ran while one was open for 6% of the time, Pallas kernels for 7%

profile of v4, /device:TPU:23, one launch (start us, length us, event | category | flops | bytes accessed | tf_op | source)
XLA Modules:
  0.0 269.1 jit_solution(15584149954856926911)
XLA Ops:
  9.8 8.8 %collective-permute-start = (bf16[512,256]{1,0:T(8,128)(2,1)S(1)}, bf16[512,256]{1,0:T(8,128)(2,1)S(1)}, u32[]{:S(2)}, u32[]{:S(2)}) collective-permute-start(bf16[512,256]{1,0:T(8,128)(2,1)S(1)} %constant_dynamic-update-slice_fusion), channel_id=1, source_target_pairs={{0,128},{32,160},{64,192},{96,224},{128,256},{160,288},{192,320},{... | collective-permute-start | bytes 786440 | tf_op jit(solution)/shard_map/ppermute | solution.py:23
  18.6 5.6 %collective-permute-start.1 = (bf16[512,256]{1,0:T(8,128)(2,1)S(1)}, bf16[512,256]{1,0:T(8,128)(2,1)S(1)}, u32[]{:S(2)}, u32[]{:S(2)}) collective-permute-start(bf16[512,256]{1,0:T(8,128)(2,1)S(1)} %constant_dynamic-update-slice_fusion), channel_id=1, source_target_pairs={{0,384},{32,416},{64,448},{96,480},{128,0},{160,32},{192,64},{224,... | collective-permute-start | bytes 786440 | tf_op jit(solution)/shard_map/ppermute | solution.py:23
  24.2 5.9 %collective-permute-done = bf16[512,256]{1,0:T(8,128)(2,1)S(1)} collective-permute-done((bf16[512,256]{1,0:T(8,128)(2,1)S(1)}, bf16[512,256]{1,0:T(8,128)(2,1)S(1)}, u32[]{:S(2)}, u32[]{:S(2)}) %collective-permute-start) | collective-permute-done | bytes 262176 | tf_op jit(solution)/shard_map/ppermute | solution.py:23
  30.0 20.6 %collective-permute-done.1 = bf16[512,256]{1,0:T(8,128)(2,1)S(1)} collective-permute-done((bf16[512,256]{1,0:T(8,128)(2,1)S(1)}, bf16[512,256]{1,0:T(8,128)(2,1)S(1)}, u32[]{:S(2)}, u32[]{:S(2)}) %collective-permute-start.1) | collective-permute-done | bytes 262176 | tf_op jit(solution)/shard_map/ppermute | solution.py:23
  53.2 4.0 %collective-permute-start.4 = (bf16[3,512,256]{2,1,0:T(8,128)(2,1)S(1)}, bf16[3,512,256]{2,1,0:T(8,128)(2,1)S(1)}, u32[]{:S(2)}, u32[]{:S(2)}) collective-permute-start(bf16[3,512,256]{2,1,0:T(8,128)(2,1)S(1)} %pad_maximum_fusion.refs_0_), channel_id=1, source_target_pairs={{0,32},{32,64},{64,96},{96,0},{128,160},{160,192},{192,224},{224,1... | collective-permute-start | bytes 2359304 | tf_op jit(solution)/shard_map/ppermute | solution.py:23
  57.3 7.2 %collective-permute-start.2 = (bf16[256,256]{1,0:T(8,128)(2,1)S(1)}, bf16[256,256]{1,0:T(8,128)(2,1)S(1)}, u32[]{:S(2)}, u32[]{:S(2)}) collective-permute-start(bf16[256,256]{1,0:T(8,128)(2,1)S(1)} %slice.464), channel_id=1, source_target_pairs={{0,128},{32,160},{64,192},{96,224},{128,256},{160,288},{192,320},{... | collective-permute-start | bytes 393224 | tf_op jit(solution)/shard_map/ppermute | solution.py:23
  66.5 6.3 %collective-permute-done.2 = bf16[256,256]{1,0:T(8,128)(2,1)S(1)} collective-permute-done((bf16[256,256]{1,0:T(8,128)(2,1)S(1)}, bf16[256,256]{1,0:T(8,128)(2,1)S(1)}, u32[]{:S(2)}, u32[]{:S(2)}) %collective-permute-start.2) | collective-permute-done | bytes 131104 | tf_op jit(solution)/shard_map/ppermute | solution.py:23
  72.8 6.1 %collective-permute-done.3 = bf16[256,256]{1,0:T(8,128)(2,1)S(1)} collective-permute-done((bf16[256,256]{1,0:T(8,128)(2,1)S(1)}, bf16[256,256]{1,0:T(8,128)(2,1)S(1)}, u32[]{:S(2)}, u32[]{:S(2)}) %collective-permute-start.3) | collective-permute-done | bytes 131104 | tf_op jit(solution)/shard_map/ppermute | solution.py:23
  80.9 8.5 %collective-permute-done.7.refs_5_ = bf16[1,512,256]{2,1,0:T(8,128)(2,1)S(1)} collective-permute-done((bf16[1,512,256]{2,1,0:T(8,128)(2,1)S(1)}, bf16[1,512,256]{2,1,0:T(8,128)(2,1)S(1)}, u32[]{:S(2)}, u32[]{:S(2)}) %collective-permute-start.7) | collective-permute-done | bytes 262176 | tf_op jit(solution)/shard_map/ppermute | solution.py:23
  93.0 4.6 %collective-permute-start.8 = (bf16[2,512,256]{2,1,0:T(8,128)(2,1)}, bf16[2,512,256]{2,1,0:T(8,128)(2,1)}, u32[]{:S(2)}, u32[]{:S(2)}) collective-permute-start(bf16[2,512,256]{2,1,0:T(8,128)(2,1)} %slice.466), channel_id=1, source_target_pairs={{0,32},{32,64},{64,96},{96,0},{128,160},{160,192},{192,224},{224,1... | collective-permute-start | bytes 1572872 | tf_op jit(solution)/shard_map/ppermute | solution.py:23
  113.1 7.7 %shard_map.110 = (bf16[256,512]{1,0:T(8,128)(2,1)S(1)}, bf16[160,256]{1,0:T(8,128)(2,1)}) custom-call(s32[2]{0:T(128)S(1)} %pad_add_fusion.1.idx_ref, bf16[32,512,256]{2,1,0:T(8,128)(2,1)} %all-gather.2.cloned.1.call-done.x_ref, f32[256,8]{1,0:T(8,128)S(1)} %pad.5.taps_ref, bf16[3,512,256]{2,1,0:T(8,128)(2,1)S(1)} %pad_maximum_fusion.refs_0_, ...), custom_call_target="tpu_custom_call" | custom-call | tf_op jit(solution)/shard_map/pallas_call | solution.py:107
  123.4 6.5 %collective-permute-start.11 = (bf16[160,256]{1,0:T(8,128)(2,1)}, bf16[160,256]{1,0:T(8,128)(2,1)S(1)}, u32[]{:S(2)}, u32[]{:S(2)}) collective-permute-start(bf16[160,256]{1,0:T(8,128)(2,1)} %get-tuple-element.26), channel_id=1, source_target_pairs={{32,64},{96,128},{160,192},{224,256},{288,320},{352,384},{416,448}... | collective-permute-start | bytes 245768 | tf_op jit(solution)/shard_map/ppermute | solution.py:28
  132.9 7.2 %collective-permute-done.11.second_ref = bf16[160,256]{1,0:T(8,128)(2,1)S(1)} collective-permute-done((bf16[160,256]{1,0:T(8,128)(2,1)}, bf16[160,256]{1,0:T(8,128)(2,1)S(1)}, u32[]{:S(2)}, u32[]{:S(2)}) %collective-permute-start.11) | collective-permute-done | bytes 81952 | tf_op jit(solution)/shard_map/ppermute | solution.py:28
  140.8 6.3 %shard_map.112 = (bf16[256,512]{1,0:T(8,128)(2,1)}, bf16[128,768]{1,0:T(8,128)(2,1)}, f32[16,128]{1,0:T(8,128)}) custom-call(s32[4]{0:T(128)} %pad_add_fusion.meta_ref, bf16[256,512]{1,0:T(8,128)(2,1)} %copy-done.1, bf16[160,256]{1,0:T(8,128)(2,1)} %copy-done.3, bf16[160,256]{1,0:T(8,128)(2,1)} %copy-done.4, f32[128,768]{1,0:T(8,128)} %get-tuple-element.27.grad_ref, ...), custom_call_target="tpu_custom_call" | custom-call | tf_op jit(solution)/shard_map/pallas_call | solution.py:376
  158.3 5.8 %shard_map.114 = (bf16[768,512]{1,0:T(8,128)(2,1)S(1)}, bf16[768,512]{1,0:T(8,128)(2,1)S(1)}, bf16[384,512]{1,0:T(8,128)(2,1)S(1)}, bf16[384,512]{1,0:T(8,128)(2,1)S(1)}, bf16[768,512]{1,0:T(8,128)(2,1)S(1)}) custom-call(s32[2]{0:T(128)S(1)} %pad_add_fusion.1.idx_ref, bf16[32,512,256]{2,1,0:T(8,128)(2,1)} %all-gather.2.cloned.1.call-done.x_ref, ...), custom_call_target="tpu_custom_call" | custom-call | tf_op jit(solution)/shard_map/pallas_call | solution.py:205
  169.5 4.3 %collective-permute-start.18 = (bf16[144,512]{1,0:T(8,128)(2,1)S(1)}, bf16[144,512]{1,0:T(8,128)(2,1)S(1)}, u32[]{:S(2)}, u32[]{:S(2)}) collective-permute-start(bf16[144,512]{1,0:T(8,128)(2,1)S(1)} %pad_maximum_fusion.4), channel_id=1, source_target_pairs={{0,32},{32,64},{64,96},{96,0},{128,160},{160,192},{192,224},{224,1... | collective-permute-start | bytes 442376 | tf_op jit(solution)/shard_map/ppermute | solution.py:23
  175.8 11.5 %collective-permute-done.18 = bf16[144,512]{1,0:T(8,128)(2,1)S(1)} collective-permute-done((bf16[144,512]{1,0:T(8,128)(2,1)S(1)}, bf16[144,512]{1,0:T(8,128)(2,1)S(1)}, u32[]{:S(2)}, u32[]{:S(2)}) %collective-permute-start.18) | collective-permute-done | bytes 147488 | tf_op jit(solution)/shard_map/ppermute | solution.py:23
  192.0 5.9 %collective-permute-start.19 = (bf16[144,512]{1,0:T(8,128)(2,1)}, bf16[144,512]{1,0:T(8,128)(2,1)S(1)}, u32[]{:S(2)}, u32[]{:S(2)}) collective-permute-start(bf16[144,512]{1,0:T(8,128)(2,1)} %get-tuple-element.111), channel_id=1, source_target_pairs={{0,128},{32,160},{64,192},{96,224},{128,256},{160,288},{192,320},{... | collective-permute-start | bytes 442376 | tf_op jit(solution)/shard_map/ppermute | solution.py:23
  203.3 9.7 %collective-permute-done.19 = bf16[144,512]{1,0:T(8,128)(2,1)S(1)} collective-permute-done((bf16[144,512]{1,0:T(8,128)(2,1)}, bf16[144,512]{1,0:T(8,128)(2,1)S(1)}, u32[]{:S(2)}, u32[]{:S(2)}) %collective-permute-start.19) | collective-permute-done | bytes 147488 | tf_op jit(solution)/shard_map/ppermute | solution.py:23
  220.6 5.6 %collective-permute-done.15 = bf16[384,512]{1,0:T(8,128)(2,1)S(1)} collective-permute-done((bf16[384,512]{1,0:T(8,128)(2,1)S(1)}, bf16[384,512]{1,0:T(8,128)(2,1)S(1)}, u32[]{:S(2)}, u32[]{:S(2)}) %collective-permute-start.15) | collective-permute-done | bytes 393248 | tf_op jit(solution)/shard_map/ppermute | solution.py:23
  226.2 4.2 %collective-permute-done.20 = bf16[384,512]{1,0:T(8,128)(2,1)S(1)} collective-permute-done((bf16[384,512]{1,0:T(8,128)(2,1)S(1)}, bf16[384,512]{1,0:T(8,128)(2,1)S(1)}, u32[]{:S(2)}, u32[]{:S(2)}) %collective-permute-start.20) | collective-permute-done | bytes 393248 | tf_op jit(solution)/shard_map/ppermute | solution.py:23
  234.0 7.3 %collective-permute-start.24 = (bf16[256,512]{1,0:T(8,128)(2,1)S(1)}, bf16[256,512]{1,0:T(8,128)(2,1)S(1)}, u32[]{:S(2)}, u32[]{:S(2)}) collective-permute-start(bf16[256,512]{1,0:T(8,128)(2,1)S(1)} %pad_maximum_fusion.3), channel_id=1, source_target_pairs={{0,384},{32,416},{64,448},{96,480},{128,0},{160,32},{192,64},{224,... | collective-permute-start | bytes 786440 | tf_op jit(solution)/shard_map/ppermute | solution.py:23
  241.2 12.9 %collective-permute-done.21 = bf16[272,512]{1,0:T(8,128)(2,1)S(1)} collective-permute-done((bf16[272,512]{1,0:T(8,128)(2,1)S(1)}, bf16[272,512]{1,0:T(8,128)(2,1)S(1)}, u32[]{:S(2)}, u32[]{:S(2)}) %collective-permute-start.21) | collective-permute-done | bytes 278560 | tf_op jit(solution)/shard_map/ppermute | solution.py:23
  254.9 5.0 %collective-permute-done.24 = bf16[256,512]{1,0:T(8,128)(2,1)S(1)} collective-permute-done((bf16[256,512]{1,0:T(8,128)(2,1)S(1)}, bf16[256,512]{1,0:T(8,128)(2,1)S(1)}, u32[]{:S(2)}, u32[]{:S(2)}) %collective-permute-start.24) | collective-permute-done | bytes 262176 | tf_op jit(solution)/shard_map/ppermute | solution.py:23
  (103 shorter events, 77.0 us)
Async XLA Ops:
  7.2 105.9 %all-gather.2.cloned.1.call-start = ((), (), s32[]{:S(2)}) async-start(), calls=%async_computation | async-start | bytes 8650752 | tf_op jit(solution)/shard_map/all_gather | solution.py:456
  9.8 20.3 %collective-permute-start = (bf16[512,256]{1,0:T(8,128)(2,1)S(1)}, bf16[512,256]{1,0:T(8,128)(2,1)S(1)}, u32[]{:S(2)}, u32[]{:S(2)}) collective-permute-start(bf16[512,256]{1,0:T(8,128)(2,1)S(1)} %constant_dynamic-update-slice_fusion), channel_id=1, source_target_pairs={{0,128},{32,160},{64,192},{96,224},{128,256},{160,288},{192,320},{... | collective-permute-start | bytes 786440 | tf_op jit(solution)/shard_map/ppermute | solution.py:23
  18.6 32.1 %collective-permute-start.1 = (bf16[512,256]{1,0:T(8,128)(2,1)S(1)}, bf16[512,256]{1,0:T(8,128)(2,1)S(1)}, u32[]{:S(2)}, u32[]{:S(2)}) collective-permute-start(bf16[512,256]{1,0:T(8,128)(2,1)S(1)} %constant_dynamic-update-slice_fusion), channel_id=1, source_target_pairs={{0,384},{32,416},{64,448},{96,480},{128,0},{160,32},{192,64},{224,... | collective-permute-start | bytes 786440 | tf_op jit(solution)/shard_map/ppermute | solution.py:23
  50.8 30.1 %collective-permute-start.6 = (bf16[3,512,256]{2,1,0:T(8,128)(2,1)S(1)}, bf16[3,512,256]{2,1,0:T(8,128)(2,1)S(1)}, u32[]{:S(2)}, u32[]{:S(2)}) collective-permute-start(bf16[3,512,256]{2,1,0:T(8,128)(2,1)S(1)} %pad_maximum_fusion.refs_0_), channel_id=1, source_target_pairs={{0,96},{32,0},{64,32},{96,64},{128,224},{160,128},{192,160},{224,1... | collective-permute-start | bytes 2359304 | tf_op jit(solution)/shard_map/ppermute | solution.py:23
  53.2 39.0 %collective-permute-start.4 = (bf16[3,512,256]{2,1,0:T(8,128)(2,1)S(1)}, bf16[3,512,256]{2,1,0:T(8,128)(2,1)S(1)}, u32[]{:S(2)}, u32[]{:S(2)}) collective-permute-start(bf16[3,512,256]{2,1,0:T(8,128)(2,1)S(1)} %pad_maximum_fusion.refs_0_), channel_id=1, source_target_pairs={{0,32},{32,64},{64,96},{96,0},{128,160},{160,192},{192,224},{224,1... | collective-permute-start | bytes 2359304 | tf_op jit(solution)/shard_map/ppermute | solution.py:23
  57.3 15.5 %collective-permute-start.2 = (bf16[256,256]{1,0:T(8,128)(2,1)S(1)}, bf16[256,256]{1,0:T(8,128)(2,1)S(1)}, u32[]{:S(2)}, u32[]{:S(2)}) collective-permute-start(bf16[256,256]{1,0:T(8,128)(2,1)S(1)} %slice.464), channel_id=1, source_target_pairs={{0,128},{32,160},{64,192},{96,224},{128,256},{160,288},{192,320},{... | collective-permute-start | bytes 393224 | tf_op jit(solution)/shard_map/ppermute | solution.py:23
  64.5 14.4 %collective-permute-start.3 = (bf16[256,256]{1,0:T(8,128)(2,1)S(1)}, bf16[256,256]{1,0:T(8,128)(2,1)S(1)}, u32[]{:S(2)}, u32[]{:S(2)}) collective-permute-start(bf16[256,256]{1,0:T(8,128)(2,1)S(1)} %slice.465), channel_id=1, source_target_pairs={{0,384},{32,416},{64,448},{96,480},{128,0},{160,32},{192,64},{224,... | collective-permute-start | bytes 393224 | tf_op jit(solution)/shard_map/ppermute | solution.py:23
  90.3 22.8 %collective-permute-start.9 = (bf16[2,512,256]{2,1,0:T(8,128)(2,1)}, bf16[2,512,256]{2,1,0:T(8,128)(2,1)S(1)}, u32[]{:S(2)}, u32[]{:S(2)}) collective-permute-start(bf16[2,512,256]{2,1,0:T(8,128)(2,1)} %pad_maximum_fusion.1), channel_id=1, source_target_pairs={{0,96},{32,0},{64,32},{96,64},{128,224},{160,128},{192,160},{224,1... | collective-permute-start | bytes 1572872 | tf_op jit(solution)/shard_map/ppermute | solution.py:23
  93.0 20.0 %collective-permute-start.8 = (bf16[2,512,256]{2,1,0:T(8,128)(2,1)}, bf16[2,512,256]{2,1,0:T(8,128)(2,1)}, u32[]{:S(2)}, u32[]{:S(2)}) collective-permute-start(bf16[2,512,256]{2,1,0:T(8,128)(2,1)} %slice.466), channel_id=1, source_target_pairs={{0,32},{32,64},{64,96},{96,0},{128,160},{160,192},{192,224},{224,1... | collective-permute-start | bytes 1572872 | tf_op jit(solution)/shard_map/ppermute | solution.py:23
  99.1 31.4 %collective-permute-start.12 = (bf16[2,144,128]{2,1,0:T(8,128)(2,1)}, bf16[2,144,128]{2,1,0:T(8,128)(2,1)}, u32[]{:S(2)}, u32[]{:S(2)}) collective-permute-start(bf16[2,144,128]{2,1,0:T(8,128)(2,1)} %slice.374), channel_id=1, source_target_pairs={{32,0},{64,32},{96,64},{128,96},{160,128},{192,160},{224,192},{256... | collective-permute-start | bytes 221192 | tf_op jit(solution)/shard_map/ppermute | solution.py:33
  101.1 12.0 %collective-permute-start.5 = (bf16[1,512,256]{2,1,0:T(8,128)(2,1)S(1)}, bf16[1,512,256]{2,1,0:T(8,128)(2,1)}, u32[]{:S(2)}, u32[]{:S(2)}) collective-permute-start(bf16[1,512,256]{2,1,0:T(8,128)(2,1)S(1)} %maximum_bitcast_fusion.refs_1_), channel_id=1, source_target_pairs={{0,32},{32,64},{64,96},{96,0},{128,160},{160,192},{192,224},{224,1... | collective-permute-start | bytes 786440 | tf_op jit(solution)/shard_map/ppermute | solution.py:23
  123.4 16.8 %collective-permute-start.11 = (bf16[160,256]{1,0:T(8,128)(2,1)}, bf16[160,256]{1,0:T(8,128)(2,1)S(1)}, u32[]{:S(2)}, u32[]{:S(2)}) collective-permute-start(bf16[160,256]{1,0:T(8,128)(2,1)} %get-tuple-element.26), channel_id=1, source_target_pairs={{32,64},{96,128},{160,192},{224,256},{288,320},{352,384},{416,448}... | collective-permute-start | bytes 245768 | tf_op jit(solution)/shard_map/ppermute | solution.py:28
  152.8 16.6 %collective-permute-start.16 = (bf16[272,512]{1,0:T(8,128)(2,1)S(1)}, bf16[272,512]{1,0:T(8,128)(2,1)S(1)}, u32[]{:S(2)}, u32[]{:S(2)}) collective-permute-start(bf16[272,512]{1,0:T(8,128)(2,1)S(1)} %get-tuple-element.38), channel_id=1, source_target_pairs={{0,32},{32,64},{64,96},{96,0},{128,160},{160,192},{192,224},{224,1... | collective-permute-start | bytes 835592 | tf_op jit(solution)/shard_map/ppermute | solution.py:23
  154.7 14.7 %collective-permute-start.17 = (bf16[272,512]{1,0:T(8,128)(2,1)S(1)}, bf16[272,512]{1,0:T(8,128)(2,1)S(1)}, u32[]{:S(2)}, u32[]{:S(2)}) collective-permute-start(bf16[272,512]{1,0:T(8,128)(2,1)S(1)} %get-tuple-element.39), channel_id=1, source_target_pairs={{0,96},{32,0},{64,32},{96,64},{128,224},{160,128},{192,160},{224,1... | collective-permute-start | bytes 835592 | tf_op jit(solution)/shard_map/ppermute | solution.py:23
  164.1 49.0 %collective-permute-start.14 = (bf16[768,512]{1,0:T(8,128)(2,1)S(1)}, bf16[768,512]{1,0:T(8,128)(2,1)}, u32[]{:S(2)}, u32[]{:S(2)}) collective-permute-start(bf16[768,512]{1,0:T(8,128)(2,1)S(1)} %get-tuple-element.34), channel_id=1, source_target_pairs={{0,32},{32,64},{64,96},{96,0},{128,160},{160,192},{192,224},{224,1... | collective-permute-start | bytes 2359304 | tf_op jit(solution)/shard_map/ppermute | solution.py:23
  167.2 48.9 %collective-permute-start.13 = (bf16[768,512]{1,0:T(8,128)(2,1)S(1)}, bf16[768,512]{1,0:T(8,128)(2,1)}, u32[]{:S(2)}, u32[]{:S(2)}) collective-permute-start(bf16[768,512]{1,0:T(8,128)(2,1)S(1)} %get-tuple-element.32), channel_id=1, source_target_pairs={{0,96},{32,0},{64,32},{96,64},{128,224},{160,128},{192,160},{224,1... | collective-permute-start | bytes 2359304 | tf_op jit(solution)/shard_map/ppermute | solution.py:23
  169.5 17.8 %collective-permute-start.18 = (bf16[144,512]{1,0:T(8,128)(2,1)S(1)}, bf16[144,512]{1,0:T(8,128)(2,1)S(1)}, u32[]{:S(2)}, u32[]{:S(2)}) collective-permute-start(bf16[144,512]{1,0:T(8,128)(2,1)S(1)} %pad_maximum_fusion.4), channel_id=1, source_target_pairs={{0,32},{32,64},{64,96},{96,0},{128,160},{160,192},{192,224},{224,1... | collective-permute-start | bytes 442376 | tf_op jit(solution)/shard_map/ppermute | solution.py:23
  173.9 17.4 %collective-permute-start.22 = (bf16[128,512]{1,0:T(8,128)(2,1)S(1)}, bf16[128,512]{1,0:T(8,128)(2,1)S(1)}, u32[]{:S(2)}, u32[]{:S(2)}) collective-permute-start(bf16[128,512]{1,0:T(8,128)(2,1)S(1)} %add_convert_fusion.3), channel_id=1, source_target_pairs={{0,96},{32,0},{64,32},{96,64},{128,224},{160,128},{192,160},{224,1... | collective-permute-start | bytes 393224 | tf_op jit(solution)/shard_map/ppermute | solution.py:23
  192.0 21.0 %collective-permute-start.19 = (bf16[144,512]{1,0:T(8,128)(2,1)}, bf16[144,512]{1,0:T(8,128)(2,1)S(1)}, u32[]{:S(2)}, u32[]{:S(2)}) collective-permute-start(bf16[144,512]{1,0:T(8,128)(2,1)} %get-tuple-element.111), channel_id=1, source_target_pairs={{0,128},{32,160},{64,192},{96,224},{128,256},{160,288},{192,320},{... | collective-permute-start | bytes 442376 | tf_op jit(solution)/shard_map/ppermute | solution.py:23
  200.0 20.5 %collective-permute-start.23 = (bf16[144,512]{1,0:T(8,128)(2,1)S(1)}, bf16[144,512]{1,0:T(8,128)(2,1)S(1)}, u32[]{:S(2)}, u32[]{:S(2)}) collective-permute-start(bf16[144,512]{1,0:T(8,128)(2,1)S(1)} %get-tuple-element.112), channel_id=1, source_target_pairs={{0,384},{32,416},{64,448},{96,480},{128,0},{160,32},{192,64},{224,... | collective-permute-start | bytes 442376 | tf_op jit(solution)/shard_map/ppermute | solution.py:23
  214.1 12.1 %collective-permute-start.15 = (bf16[384,512]{1,0:T(8,128)(2,1)S(1)}, bf16[384,512]{1,0:T(8,128)(2,1)S(1)}, u32[]{:S(2)}, u32[]{:S(2)}) collective-permute-start(bf16[384,512]{1,0:T(8,128)(2,1)S(1)} %add_convert_fusion.1), channel_id=1, source_target_pairs={{0,32},{32,64},{64,96},{96,0},{128,160},{160,192},{192,224},{224,1... | collective-permute-start | bytes 1179656 | tf_op jit(solution)/shard_map/ppermute | solution.py:23
  217.2 13.3 %collective-permute-start.20 = (bf16[384,512]{1,0:T(8,128)(2,1)S(1)}, bf16[384,512]{1,0:T(8,128)(2,1)S(1)}, u32[]{:S(2)}, u32[]{:S(2)}) collective-permute-start(bf16[384,512]{1,0:T(8,128)(2,1)S(1)} %add_convert_fusion), channel_id=1, source_target_pairs={{0,96},{32,0},{64,32},{96,64},{128,224},{160,128},{192,160},{224,1... | collective-permute-start | bytes 1179656 | tf_op jit(solution)/shard_map/ppermute | solution.py:23
  232.0 22.1 %collective-permute-start.21 = (bf16[272,512]{1,0:T(8,128)(2,1)S(1)}, bf16[272,512]{1,0:T(8,128)(2,1)S(1)}, u32[]{:S(2)}, u32[]{:S(2)}) collective-permute-start(bf16[272,512]{1,0:T(8,128)(2,1)S(1)} %pad_maximum_fusion.2), channel_id=1, source_target_pairs={{0,128},{32,160},{64,192},{96,224},{128,256},{160,288},{192,320},{... | collective-permute-start | bytes 835592 | tf_op jit(solution)/shard_map/ppermute | solution.py:23
  234.0 26.0 %collective-permute-start.24 = (bf16[256,512]{1,0:T(8,128)(2,1)S(1)}, bf16[256,512]{1,0:T(8,128)(2,1)S(1)}, u32[]{:S(2)}, u32[]{:S(2)}) collective-permute-start(bf16[256,512]{1,0:T(8,128)(2,1)S(1)} %pad_maximum_fusion.3), channel_id=1, source_target_pairs={{0,384},{32,416},{64,448},{96,480},{128,0},{160,32},{192,64},{224,... | collective-permute-start | bytes 786440 | tf_op jit(solution)/shard_map/ppermute | solution.py:23
  (8 other events, 173.5 us)
Sparse Core Ops, SparseCore 0:
  10.1 101.4 all-gather.1
